TPU v7x, 128 devices: a whole 4x4x4 slice. The times are simulated.
128 devices in a mesh: ctx: 32 (over y, z_lo, x), ep: 4 (over z_hi, core).
Axes of the slice: x: 4, y: 4, z: 4 (z_hi: 2, z_lo: 2; z = z_hi * 2 + z_lo), core: 2. Of those that a mesh axis runs over, the one named last changes fastest.
Arguments:
- block_input_rows: bfloat16 [16384, 4096], P(('ctx', 'ep')), may hold values from -6 to 6
- output_gradient: bfloat16 [16384, 4096], P(('ctx', 'ep')), may hold values from -12 to 12
- expert_choice_index: int32 [16384, 8], P(('ctx', 'ep')), may hold values from 0 to 127, all different within a row; in each aligned block of 128 rows (0 to 127, 128 to 255, ...) at most 9 rows name the same one
- routing_weight_rows: float32 [16384, 8], P(('ctx', 'ep')), may hold values from 0.03 to 0.5
- frozen_gate_weight: bfloat16 [128, 4096, 768], P(('ctx', 'ep')), may hold values from -0.09375 to 0.09375
- frozen_up_weight: bfloat16 [128, 4096, 768], P(('ctx', 'ep')), may hold values from -0.09375 to 0.09375
- frozen_down_weight: bfloat16 [128, 768, 4096], P(('ctx', 'ep')), may hold values from -0.21875 to 0.21875
- gate_adapter_inmap: bfloat16 [128, 16, 4096], P(('ctx', 'ep')), may hold values from -0.09375 to 0.09375
- gate_adapter_outmap: bfloat16 [128, 16, 768], P(('ctx', 'ep')), may hold values from -0.21875 to 0.21875
- up_adapter_inmap: bfloat16 [128, 16, 4096], P(('ctx', 'ep')), may hold values from -0.09375 to 0.09375
- up_adapter_outmap: bfloat16 [128, 16, 768], P(('ctx', 'ep')), may hold values from -0.21875 to 0.21875
- down_adapter_inmap: bfloat16 [128, 16, 768], P(('ctx', 'ep')), may hold values from -0.21875 to 0.21875
- down_adapter_outmap: bfloat16 [128, 16, 4096], P(('ctx', 'ep')), may hold values from -0.09375 to 0.09375
- stored_gate_preact: bfloat16 [128, 1152, 768], P(('ctx', 'ep')), may hold values from -8 to 8
- stored_up_preact: bfloat16 [128, 1152, 768], P(('ctx', 'ep')), may hold values from -6 to 6
Outputs:
- grad_in: bfloat16 [16384, 4096], P(('ctx', 'ep'))
- gate_input_gradient: bfloat16 [128, 16, 4096], P(('ctx', 'ep'))
- gate_output_gradient: bfloat16 [128, 16, 768], P(('ctx', 'ep'))
- up_input_gradient: bfloat16 [128, 16, 4096], P(('ctx', 'ep'))
- up_output_gradient: bfloat16 [128, 16, 768], P(('ctx', 'ep'))
- down_input_gradient: bfloat16 [128, 16, 768], P(('ctx', 'ep'))
- down_output_gradient: bfloat16 [128, 16, 4096], P(('ctx', 'ep'))
Inputs may be any that keep to these rules, and one draw needn't show every extreme that they name: `expert_choice_index`: A token names 8 different experts. Among the tokens of one device, an expert is named by at most 9 of them, and in every draw some expert by exactly 9.
All inputs are finite; a program needn't handle non-finite values.
Results may differ from a plain program's by a relative error of at most 0.0065.
Values may be sent and summed in bfloat16 or wider, within the bound.
A program may use at most 256 MiB of HBM per device.

v0:
```python
import jax
import jax.numpy as jnp
from jax import lax
from jax.sharding import PartitionSpec as P

adapter_scale = 2.0


def contract_matrices(left_mat, right_mat, left_axis, right_axis):
    return lax.dot_general(
        left_mat,
        right_mat,
        (((left_axis,), (right_axis,)), ((), ())),
        preferred_element_type=jnp.float32,
    )


def expert_backward(
    gathered_input_rows,
    gathered_gradient_rows,
    gate_pre,
    up_pre,
    frozen_gate_weight,
    frozen_up_weight,
    frozen_down_weight,
    gate_adapter_input,
    gate_out,
    up_adapter_input,
    up_out,
    down_adapter_input,
    down_adapter_output,
):
    rank_width = gate_adapter_input.shape[0]
    gate_value = gate_pre.astype(jnp.float32)
    up_value = up_pre.astype(jnp.float32)
    sigmoid_gate = jax.nn.sigmoid(gate_value)
    silu_gate = gate_value * sigmoid_gate
    hidden_activation = (silu_gate * up_value).astype(jnp.bfloat16)
    down_adapter_delta = contract_matrices(hidden_activation, down_adapter_input, 1, 1).astype(
        jnp.bfloat16
    )
    adapter_gradient = contract_matrices(gathered_gradient_rows, down_adapter_output, 1, 1).astype(
        jnp.bfloat16
    )
    down_output_gradient = adapter_scale * contract_matrices(
        down_adapter_delta, gathered_gradient_rows, 0, 0
    )
    down_input_gradient = adapter_scale * contract_matrices(
        adapter_gradient, hidden_activation, 0, 0
    )
    hidden_gradient_rows = contract_matrices(
        gathered_gradient_rows, frozen_down_weight, 1, 1
    ) + adapter_scale * contract_matrices(adapter_gradient, down_adapter_input, 1, 0)
    gate_gradient_rows = (
        hidden_gradient_rows * up_value * sigmoid_gate * (1.0 + gate_value * (1.0 - sigmoid_gate))
    ).astype(jnp.bfloat16)
    up_gradient_rows = (hidden_gradient_rows * silu_gate).astype(jnp.bfloat16)
    both_inputs = jnp.concatenate([gate_adapter_input, up_adapter_input], axis=0)
    both_deltas = contract_matrices(gathered_input_rows, both_inputs, 1, 1).astype(jnp.bfloat16)
    gate_adapter_delta = both_deltas[:, :rank_width]
    up_adapter_delta = both_deltas[:, rank_width:]
    gate_output_gradient = adapter_scale * contract_matrices(
        gate_adapter_delta, gate_gradient_rows, 0, 0
    )
    up_output_gradient = adapter_scale * contract_matrices(up_adapter_delta, up_gradient_rows, 0, 0)
    gate_backward_rows = contract_matrices(gate_gradient_rows, gate_out, 1, 1).astype(jnp.bfloat16)
    up_backward_rows = contract_matrices(up_gradient_rows, up_out, 1, 1).astype(jnp.bfloat16)
    both_backward = jnp.concatenate([gate_backward_rows, up_backward_rows], axis=1)
    both_input_gradients = adapter_scale * contract_matrices(
        both_backward, gathered_input_rows, 0, 0
    )
    gate_input_gradient = both_input_gradients[:rank_width]
    up_input_gradient = both_input_gradients[rank_width:]
    left_joined = jnp.concatenate([gate_gradient_rows, up_gradient_rows, both_backward], axis=1)
    scaled_inputs = (both_inputs.astype(jnp.float32) * adapter_scale).astype(jnp.bfloat16)
    right_joined = jnp.concatenate([frozen_gate_weight, frozen_up_weight, scaled_inputs.T], axis=1)
    scattered_output_rows = contract_matrices(left_joined, right_joined, 1, 1)
    expert_outcomes = (
        gate_input_gradient.astype(jnp.bfloat16),
        gate_output_gradient.astype(jnp.bfloat16),
        up_input_gradient.astype(jnp.bfloat16),
        up_output_gradient.astype(jnp.bfloat16),
        down_input_gradient.astype(jnp.bfloat16),
        down_output_gradient.astype(jnp.bfloat16),
    )
    return (scattered_output_rows.astype(jnp.bfloat16), expert_outcomes)


def local(
    block_input_rows,
    output_gradient,
    expert_choice_index,
    routing_weight_rows,
    frozen_gate_weight,
    frozen_up_weight,
    frozen_down_weight,
    gate_adapter_inmap,
    gate_adapter_outmap,
    up_adapter_inmap,
    up_adapter_outmap,
    down_adapter_inmap,
    down_adapter_outmap,
    stored_gate_preact,
    stored_up_preact,
):
    tok_rows, model_width = block_input_rows.shape
    top_count = expert_choice_index.shape[1]
    ctx_count = lax.axis_size("ctx")
    ep_count = lax.axis_size("ep")
    devices = ctx_count * ep_count
    local_exp = frozen_gate_weight.shape[0]
    experts = local_exp * devices
    slot_count = stored_gate_preact.shape[1]
    capacity = slot_count // devices
    pick_count = tok_rows * top_count
    flat_ids = expert_choice_index.reshape(pick_count)
    onehot = (flat_ids[:, None] == jnp.arange(experts, dtype=jnp.int32)[None, :]).astype(
        jnp.bfloat16
    )
    pick_iota = jnp.arange(pick_count, dtype=jnp.int32)
    lower_mask = (pick_iota[:, None] >= pick_iota[None, :]).astype(jnp.bfloat16)
    running = jnp.dot(lower_mask, onehot, preferred_element_type=jnp.float32)
    slot_num = (jnp.sum(onehot.astype(jnp.float32) * running, axis=1) - 1.0).astype(jnp.int32)
    target = flat_ids * capacity + slot_num
    source = jnp.full((experts * capacity,), pick_count, jnp.int32).at[target].set(pick_iota)
    filled = source < pick_count
    pick_safe = jnp.minimum(source, pick_count - 1)
    token_index = jnp.where(filled, pick_safe // top_count, tok_rows)
    weight_flat = routing_weight_rows.reshape(pick_count)
    slot_weight = jnp.where(filled, weight_flat[pick_safe], 0.0)
    zero_row = jnp.zeros((1, model_width), jnp.bfloat16)
    padded_input = jnp.concatenate([block_input_rows, zero_row], axis=0)
    padded_grad = jnp.concatenate([output_gradient, zero_row], axis=0)
    send_rows = padded_input[token_index].reshape(experts, capacity, model_width)
    send_grad = (
        (slot_weight[:, None] * padded_grad[token_index].astype(jnp.float32))
        .astype(jnp.bfloat16)
        .reshape(experts, capacity, model_width)
    )
    got_rows, got_grad = (
        lax.all_to_all(send_rows, ("ctx", "ep"), split_axis=0, concat_axis=1, tiled=True),
        lax.all_to_all(send_grad, ("ctx", "ep"), split_axis=0, concat_axis=1, tiled=True),
    )
    scattered_output_rows, expert_outcomes = jax.vmap(expert_backward)(
        got_rows,
        got_grad,
        stored_gate_preact,
        stored_up_preact,
        frozen_gate_weight,
        frozen_up_weight,
        frozen_down_weight,
        gate_adapter_inmap,
        gate_adapter_outmap,
        up_adapter_inmap,
        up_adapter_outmap,
        down_adapter_inmap,
        down_adapter_outmap,
    )
    returned = lax.all_to_all(
        scattered_output_rows, ("ctx", "ep"), split_axis=1, concat_axis=0, tiled=True
    )
    returned_flat = returned.reshape(experts * capacity, model_width)
    picked = returned_flat[target].reshape(tok_rows, top_count, model_width)
    grad_in = jnp.sum(picked.astype(jnp.float32), axis=1).astype(jnp.bfloat16)
    return (
        grad_in,
        expert_outcomes[0],
        expert_outcomes[1],
        expert_outcomes[2],
        expert_outcomes[3],
        expert_outcomes[4],
        expert_outcomes[5],
    )


def solution(mesh):
    in_specs = (
        P(("ctx", "ep"), None),
        P(("ctx", "ep"), None),
        P(("ctx", "ep"), None),
        P(("ctx", "ep"), None),
        P(("ctx", "ep"), None, None),
        P(("ctx", "ep"), None, None),
        P(("ctx", "ep"), None, None),
        P(("ctx", "ep"), None, None),
        P(("ctx", "ep"), None, None),
        P(("ctx", "ep"), None, None),
        P(("ctx", "ep"), None, None),
        P(("ctx", "ep"), None, None),
        P(("ctx", "ep"), None, None),
        P(("ctx", "ep"), None, None),
        P(("ctx", "ep"), None, None),
    )
    out_specs = (
        P(("ctx", "ep"), None),
        P(("ctx", "ep"), None, None),
        P(("ctx", "ep"), None, None),
        P(("ctx", "ep"), None, None),
        P(("ctx", "ep"), None, None),
        P(("ctx", "ep"), None, None),
        P(("ctx", "ep"), None, None),
    )
    return jax.shard_map(local, mesh=mesh, in_specs=in_specs, out_specs=out_specs, check_vma=False)
```

profile of v0, /device:TPU:12, one launch (start us, length us, event | category | flops | bytes accessed | tf_op | source)
XLA Modules:
  0.0 794.7 jit_solution(17630708598642614224)
XLA Ops:
  13.4 7.9 gather_fusion.1
  21.3 17.6 %reshape.237 = f32[128,9,4096]{2,1,0:T(8,128)} reshape(bf16[1152,4096]{1,0:T(8,128)(2,1)} %gather_fusion.1) | data formatting | bytes 28311552 | tf_op jit(solution)/shard_map/convert_element_type | solution.py:136
  38.9 18.0 %multiply_convert_fusion = bf16[128,9,4096]{2,1,0:T(8,128)(2,1)} fusion(f32[128,9,4096]{2,1,0:T(8,128)} %reshape.237, f32[128,9]{1,0:T(8,128)S(1)} %mul.98), kind=kLoop, calls=%fused_computation.5 | loop fusion | flops 9437184 | bytes 28316160 | tf_op jit(solution)/shard_map/convert_element_type | solution.py:137
  56.9 10.8 %all-to-all-start = ((bf16[128,9,4096]{2,1,0:T(8,128)(2,1)}), bf16[128,9,4096]{2,1,0:T(8,128)(2,1)}, u32[]{:S(2)}, u32[]{:S(2)}) async-start(bf16[128,9,4096]{2,1,0:T(8,128)(2,1)} %multiply_convert_fusion), calls=%async_computation | async-start | bytes 33554432 | tf_op jit(solution)/shard_map/all_to_all | solution.py:142
  67.9 8.0 %gather_fusion.3 = bf16[1152,4096]{1,0:T(8,128)(2,1)} fusion(bf16[129,4096]{1,0:T(8,128)(2,1)S(1)} %concatenate.32, s32[2048]{0:T(1024)S(1)} %get-tuple-element.14), kind=kCustom, calls=%fused_computation.3 | custom fusion | bytes 18878976 | tf_op jit(solution)/shard_map/gather | solution.py:134
  76.0 15.0 %reshape.231 = bf16[128,9,4096]{2,1,0:T(8,128)(2,1)} reshape(bf16[1152,4096]{1,0:T(8,128)(2,1)} %gather_fusion.3) | data formatting | bytes 18874368 | tf_op jit(solution)/shard_map/reshape | solution.py:134
  91.0 212.3 %all-to-all-done = bf16[128,9,4096]{2,1,0:T(8,128)(2,1)} async-done(((bf16[128,9,4096]{2,1,0:T(8,128)(2,1)}), bf16[128,9,4096]{2,1,0:T(8,128)(2,1)}, u32[]{:S(2)}, u32[]{:S(2)}) %all-to-all-start) | async-done | bytes 9437216 | tf_op jit(solution)/shard_map/all_to_all | solution.py:142
  303.3 17.5 %all-to-all-start.2 = ((bf16[128,9,4096]{2,1,0:T(8,128)(2,1)}), bf16[128,9,4096]{2,1,0:T(8,128)(2,1)}, u32[]{:S(2)}, u32[]{:S(2)}) async-start(bf16[128,9,4096]{2,1,0:T(8,128)(2,1)} %reshape.231), calls=%async_computation.2 | async-start | bytes 33554432 | tf_op jit(solution)/shard_map/all_to_all | solution.py:141
  327.6 15.6 %reshape.218 = bf16[1152,4096]{1,0:T(8,128)(2,1)} reshape(bf16[128,9,4096]{2,1,0:T(8,128)(2,1)} %all-to-all-done) | data formatting | bytes 18874368 | tf_op jit(solution)/shard_map/reshape.2
  343.2 6.4 convolution_convert_fusion.5
  349.7 10.9 %fusion.5 = f32[1152,768]{0,1:T(8,128)S(1)} fusion(bf16[1152,4096]{1,0:T(8,128)(2,1)S(1)} %copy-done.3, bf16[1,768,4096]{2,1,0:T(8,128)(2,1)} %param.21), kind=kOutput, calls=%fused_computation.15 | convolution fusion | flops 7247757312 | bytes 19267584 | tf_op jit(solution)/shard_map/vmap()/dot_general | solution.py:10
  365.5 24.0 %fusion.4 = bf16[1,1152,4096]{2,1,0:T(8,128)(2,1)} fusion(bf16[1,4096,32]{2,1,0:T(8,128)(2,1)S(1)} %copy.43, bf16[1,4096,768]{2,1,0:T(8,128)(2,1)} %param.20, bf16[1,4096,768]{2,1,0:T(8,128)(2,1)} %param.19, bf16[1,1152,16]{1,2,0:T(8,128)(2,1)S(1)} %fusion.30, bf16[1,1152,16]{1,2,0:T(8,128)(2,1)S(1)} %fusion.29, bf16[1,1152,768]{1,2,0:T(8,128)(2,1)} %copy-done.4, ...), kind=kOutput, calls=%fused_computation.12 | convolution fusion | flops 14855208960 | bytes 25894912 | tf_op jit(solution)/shard_map/vmap()/dot_general | solution.py:10
  389.5 22.4 %copy.49 = bf16[1,1152,4096]{2,0,1:T(2,128)(2,1)} copy(bf16[1,1152,4096]{2,1,0:T(8,128)(2,1)} %fusion.4) | data formatting | bytes 18874368 | tf_op jit(solution)/shard_map/vmap()/convert_element_type | solution.py:86
  412.4 58.8 %reduce.1 = bf16[1152,4096]{1,0:T(8,128)(2,1)} reduce(bf16[1152,1,4096]{2,1,0:T(2,128)(2,1)} %bitcast.110, bf16[]{:T(256)} %broadcast.135), dimensions={1}, to_apply=%bitcast.107.reduce_sub_computation | reduce | bytes 18874370
  471.1 16.4 %reshape.284 = bf16[128,2,18432]{2,1,0:T(2,128)(2,1)} reshape(bf16[1152,4096]{1,0:T(8,128)(2,1)} %reduce.1) | data formatting | bytes 18874368
  487.5 66.0 %all-to-all-done.2 = bf16[128,9,4096]{2,1,0:T(8,128)(2,1)} async-done(((bf16[128,9,4096]{2,1,0:T(8,128)(2,1)}), bf16[128,9,4096]{2,1,0:T(8,128)(2,1)}, u32[]{:S(2)}, u32[]{:S(2)}) %all-to-all-start.2) | async-done | bytes 9437216 | tf_op jit(solution)/shard_map/all_to_all | solution.py:141
  553.6 19.3 %all-to-all-start.1 = ((bf16[128,2,18432]{2,1,0:T(2,128)(2,1)}), bf16[128,2,18432]{2,1,0:T(2,128)(2,1)}, u32[]{:S(2)}, u32[]{:S(2)}) async-start(bf16[128,2,18432]{2,1,0:T(2,128)(2,1)} %reshape.284), calls=%async_computation.1 | async-start | bytes 18874368 | tf_op jit(solution)/shard_map/all_to_all | solution.py:159
  572.9 15.7 %reshape.232 = bf16[1152,4096]{1,0:T(8,128)(2,1)} reshape(bf16[128,9,4096]{2,1,0:T(8,128)(2,1)} %all-to-all-done.2) | data formatting | bytes 18874368 | tf_op jit(solution)/shard_map/reshape.40
  588.6 6.7 fusion.28
  608.8 97.3 %all-to-all-done.1 = bf16[128,2,18432]{2,1,0:T(2,128)(2,1)} async-done(((bf16[128,2,18432]{2,1,0:T(2,128)(2,1)}), bf16[128,2,18432]{2,1,0:T(2,128)(2,1)}, u32[]{:S(2)}, u32[]{:S(2)}) %all-to-all-start.1) | async-done | bytes 9437216 | tf_op jit(solution)/shard_map/all_to_all | solution.py:159
  706.1 39.3 %reshape.285 = bf16[1152,1,4096]{2,1,0:T(2,128)(2,1)} reshape(bf16[128,2,18432]{2,1,0:T(2,128)(2,1)} %all-to-all-done.1) | data formatting | bytes 18874368
  745.5 18.4 %copy.48 = bf16[1,1152,4096]{2,1,0:T(8,128)(2,1)} copy(bf16[1,1152,4096]{2,0,1:T(2,128)(2,1)} %bitcast.109) | data formatting | bytes 18874368
  763.8 20.3 %gather_fusion.2 = bf16[1024,4096]{1,0:T(8,128)(2,1)} fusion(bf16[1152,4096]{1,0:T(8,128)(2,1)} %bitcast.108, s32[1024]{0:T(1024)S(1)} %broadcast_clamp_fusion), kind=kCustom, calls=%fused_computation.2 | custom fusion | bytes 16781312 | tf_op jit(solution)/shard_map/gather | solution.py:163
  784.2 10.1 %bitcast_reduce_fusion = bf16[128,4096]{1,0:T(8,128)(2,1)} fusion(bf16[1024,4096]{1,0:T(8,128)(2,1)} %gather_fusion.2), kind=kLoop, calls=%fused_computation.14 | loop fusion | flops 3670016 | bytes 9437184 | tf_op jit(solution)/shard_map/reduce_sum | solution.py:164
  (74 shorter events, 38.2 us)
Async XLA Ops:
  0.6 342.6 %copy-start = (bf16[1,16,4096]{2,1,0:T(8,128)(2,1)S(1)}, bf16[1,16,4096]{2,1,0:T(8,128)(2,1)}, u32[]{:S(2)}) copy-start(bf16[1,16,4096]{2,1,0:T(8,128)(2,1)} %param.27) | copy-start | bytes 393220
  0.6 12.6 %copy-start.10 = (bf16[128,4096]{1,0:T(8,128)(2,1)S(1)}, bf16[128,4096]{1,0:T(8,128)(2,1)}, u32[]{:S(2)}) copy-start(bf16[128,4096]{1,0:T(8,128)(2,1)} %param.16) | copy-start | bytes 3145732
  3.2 4.4 copy-start.17
  56.9 10.9 %copy-start.11 = (bf16[128,4096]{1,0:T(8,128)(2,1)S(1)}, bf16[128,4096]{1,0:T(8,128)(2,1)}, u32[]{:S(2)}) copy-start(bf16[128,4096]{1,0:T(8,128)(2,1)} %param.15) | copy-start | bytes 3145732
  56.9 246.4 %all-to-all-start = ((bf16[128,9,4096]{2,1,0:T(8,128)(2,1)}), bf16[128,9,4096]{2,1,0:T(8,128)(2,1)}, u32[]{:S(2)}, u32[]{:S(2)}) async-start(bf16[128,9,4096]{2,1,0:T(8,128)(2,1)} %multiply_convert_fusion), calls=%async_computation | async-start | bytes 33554432 | tf_op jit(solution)/shard_map/all_to_all | solution.py:142
  91.0 229.9 %copy-start.7 = (bf16[1,1152,768]{2,1,0:T(8,128)(2,1)S(1)}, bf16[1,1152,768]{2,1,0:T(8,128)(2,1)}, u32[]{:S(2)}) copy-start(bf16[1,1152,768]{2,1,0:T(8,128)(2,1)} %param.29) | copy-start | bytes 5308420
  303.3 250.2 %all-to-all-start.2 = ((bf16[128,9,4096]{2,1,0:T(8,128)(2,1)}), bf16[128,9,4096]{2,1,0:T(8,128)(2,1)}, u32[]{:S(2)}, u32[]{:S(2)}) async-start(bf16[128,9,4096]{2,1,0:T(8,128)(2,1)} %reshape.231), calls=%async_computation.2 | async-start | bytes 33554432 | tf_op jit(solution)/shard_map/all_to_all | solution.py:141
  320.9 6.2 copy-start.12
  320.9 6.2 copy-start.13
  343.2 6.4 copy-start.3
  349.6 11.0 %copy-start.8 = (bf16[1,1152,768]{1,2,0:T(8,128)(2,1)S(1)}, bf16[1,1152,768]{1,2,0:T(8,128)(2,1)}, u32[]{:S(2)}) copy-start(bf16[1,1152,768]{1,2,0:T(8,128)(2,1)} %copy.41) | copy-start | bytes 5308420
  349.6 11.0 %copy-start.9 = (bf16[1,1152,768]{1,2,0:T(8,128)(2,1)S(1)}, bf16[1,1152,768]{1,2,0:T(8,128)(2,1)}, u32[]{:S(2)}) copy-start(bf16[1,1152,768]{1,2,0:T(8,128)(2,1)} %copy.42) | copy-start | bytes 5308420
  349.6 11.0 %copy-start.16 = (bf16[1,16,768]{2,1,0:T(8,128)(2,1)S(1)}, bf16[1,16,768]{2,1,0:T(8,128)(2,1)}, u32[]{:S(2)}) copy-start(bf16[1,16,768]{2,1,0:T(8,128)(2,1)} %param.26) | copy-start | bytes 73732
  360.6 3.9 copy-start.14
  360.6 4.5 copy-start.15
  363.3 1.2 copy-start.6
  363.3 1.8 copy-start.4
  487.5 85.4 %copy-start.18 = (s32[1024,1]{0,1:T(1,128)S(1)}, s32[1024,1]{0,1:T(1,128)}, u32[]{:S(2)}) copy-start(s32[1024,1]{0,1:T(1,128)} %copy-done.17) | copy-start | bytes 12292
  553.6 152.6 %all-to-all-start.1 = ((bf16[128,2,18432]{2,1,0:T(2,128)(2,1)}), bf16[128,2,18432]{2,1,0:T(2,128)(2,1)}, u32[]{:S(2)}, u32[]{:S(2)}) async-start(bf16[128,2,18432]{2,1,0:T(2,128)(2,1)} %reshape.284), calls=%async_computation.1 | async-start | bytes 18874368 | tf_op jit(solution)/shard_map/all_to_all | solution.py:159
  588.6 9.4 %copy-start.5 = (bf16[1,1152,768]{1,2,0:T(8,128)(2,1)S(1)}, bf16[1,1152,768]{1,2,0:T(8,128)(2,1)}, u32[]{:S(2)}) copy-start(bf16[1,1152,768]{1,2,0:T(8,128)(2,1)} %copy-done.4) | copy-start | bytes 5308420
  588.6 11.8 %copy-start.2 = (bf16[1152,4096]{1,0:T(8,128)(2,1)S(1)}, bf16[1152,4096]{1,0:T(8,128)(2,1)}, u32[]{:S(2)}) copy-start(bf16[1152,4096]{1,0:T(8,128)(2,1)} %reshape.232) | copy-start | bytes 28311556
  763.8 30.5 %copy-start.1 = (bf16[1,16,4096]{2,1,0:T(8,128)(2,1)S(1)}, bf16[1,16,4096]{2,1,0:T(8,128)(2,1)}, u32[]{:S(2)}) copy-start(bf16[1,16,4096]{2,1,0:T(8,128)(2,1)} %param.27) | copy-start | bytes 393220
where the time goes:
time: 804 us; the launch traced here: 795 us
  waiting for transfers between devices  376 us (47%)
  local copies, waits for them, and re-layouts  217 us (27%)
  other arithmetic  87.7 us (11%)
  matrix products  64.8 us (8%)
  starting transfers between devices  47.7 us (6%)
    all_to_all x1, waiting for transfers between devices, local(): lax.all_to_all(send_grad, ('ctx', 'ep'), split_axis=0, concat_axis=1, til...  212 us
    all_to_all x1, waiting for transfers between devices, local(): lax.all_to_all(scattered_output_rows, ('ctx', 'ep'), split_axis=1, concat...  97.3 us
    unnamed x47, local copies, waits for them, and re-layouts  83.9 us
    all_to_all x1, waiting for transfers between devices, local(): lax.all_to_all(send_rows, ('ctx', 'ep'), split_axis=0, concat_axis=1, til...  66 us
    dot_general x12, matrix products, contract_matrices(): lax.dot_general(left_mat, right_mat, (((left_axis,), (right_axis,)), ((),...  64.1 us
    unnamed x1, other arithmetic  58.8 us
    another operation x2, local copies, waits for them, and re-layouts  31.3 us
    convert_element_type x1, local copies, waits for them, and re-layouts, expert_backward(): return (scattered_output_rows.astype(jnp.bfloat16), expert_outcomes)  22.4 us
  transfers between devices with their start and end apart: 3, of which 3 were waited for; matrix products, arithmetic and copies ran while one was open for 28% of the time, Pallas kernels for 0%

commit v1 on v0

v1 whole, which is shorter than its diff:
```python
import functools

import jax
import jax.numpy as jnp
from jax import lax
from jax.experimental import pallas as pl
from jax.experimental.pallas import tpu as pltpu
from jax.sharding import PartitionSpec as P

MESH = pl.DeviceIdType.MESH
ROLES = ((0, 1, 2), (1, 2, 0), (2, 0, 1))
WID = (1280, 1280, 1536)
OFF = (0, 1280, 2560)
CHUNK = 256
F32 = jnp.float32
BF16 = jnp.bfloat16
adapter_scale = 2.0


def coords():
    c = lax.axis_index("ctx")
    e = lax.axis_index("ep")
    x = lax.rem(c, 4)
    y = c // 8
    z = (e // 2) * 2 + lax.rem(c // 4, 2)
    return (x, y, z), lax.rem(e, 2)


def device(pos, core):
    x, y, z = pos
    return ((y * 2 + lax.rem(z, 2)) * 4 + x, (z // 2) * 2 + core)


def moved(pos, axis, d):
    out = list(pos)
    out[axis] = lax.rem(pos[axis] + d, 4)
    return tuple(out)


def greet(pos, core):
    barrier = pltpu.get_barrier_semaphore()
    other = 1 - core
    peers = [device(pos, other)]
    for axis in range(3):
        for d in (1, 2, 3):
            peers.append(device(moved(pos, axis, d), core))
            peers.append(device(moved(pos, axis, d), other))
    for peer in peers:
        pl.semaphore_signal(barrier, inc=1, device_id=peer, device_id_type=MESH)
    return barrier, len(peers)


def remote(src, dst, ssem, rsem, dev):
    return pltpu.make_async_remote_copy(
        src_ref=src, dst_ref=dst, send_sem=ssem, recv_sem=rsem, device_id=dev, device_id_type=MESH
    )


def expert_ids(j, shape):
    i = lax.broadcasted_iota(jnp.int32, shape, 0)
    v = [None] * 3
    a, b, c = ROLES[j]
    v[a] = i // 32
    v[b] = (i // 8) % 4
    v[c] = (i // 2) % 4
    k = i % 2
    x, y, z = v
    return ((y * 2 + z % 2) * 4 + x) * 4 + (z // 2) * 2 + k


def main_at(ref, j, b, c, k):
    ra, rb, rc = ROLES[j]
    idx = [None] * 3
    idx[ra] = slice(None)
    idx[rb] = b
    idx[rc] = c
    return ref.at[idx[0], idx[1], idx[2], k, :, pl.ds(OFF[j], WID[j])]


def cols(j):
    return [(s, CHUNK) for s in range(0, WID[j], CHUNK)]


def dispatch_kernel(*refs):
    ids_ref, wt_ref, g_ref, x_ref = refs[:4]
    outs = refs[4:13]
    gmain, xmain = outs[0], outs[1]
    tails = (outs[2:5], outs[5:8])
    masks = outs[8]
    scratch = refs[13:]
    ag = scratch[0:3]
    send2 = scratch[3:6]
    recv2 = scratch[6:9]
    send2t = scratch[9:12]
    recv2t = scratch[12:15]
    tab, tabr, pm, wmain, wtail = scratch[15:20]
    sems = scratch[20]
    mains = (gmain, xmain)
    data = (g_ref, x_ref)
    pos, core = coords()
    other = 1 - core
    barrier, count = greet(pos, core)

    row = lax.broadcasted_iota(jnp.int32, (128, 128), 0)
    lane = lax.broadcasted_iota(jnp.int32, (128, 128), 1)
    strict = (row < lane).astype(BF16)
    for j in range(3):
        eid = expert_ids(j, (128, 128))
        hit = jnp.zeros((128, 128), F32)
        wgt = jnp.zeros((128, 128), F32)
        for k in range(8):
            same = eid == ids_ref[k : k + 1, :]
            hit = hit + jnp.where(same, 1.0, 0.0)
            wgt = wgt + jnp.where(same, wt_ref[k : k + 1, :], 0.0)
        rank = jnp.dot(hit.astype(BF16), strict, preferred_element_type=F32)
        code = jnp.where(hit > 0.5, rank, -1.0)
        tab[j, :, 0] = code.reshape(4, 32, 128)
        tab[j, :, 1] = wgt.reshape(4, 32, 128)
    pl.semaphore_wait(barrier, count)

    def sem(i):
        return sems.at[i]

    def n1(p, j):
        return p * 3 + j

    def nt(j):
        return 6 + j

    def n2(p, j, t):
        return 9 + (p * 3 + j) * 2 + t

    def n3(p, j, t):
        return 21 + (p * 3 + j) * 2 + t

    RB = 33

    def stage1(p):
        for j in range(3):
            ra = ROLES[j][0]
            me = pos[ra]
            src = data[p].at[:, pl.ds(OFF[j], WID[j])]
            for d in (1, 2, 3):
                dev = device(moved(pos, ra, d), core)
                if p == 0:
                    to = lax.rem(me + d, 4)
                    remote(tab.at[j, to], tabr.at[j, me], sem(nt(j)), sem(RB + nt(j)), dev).start()
                remote(src, ag[j].at[p, me], sem(n1(p, j)), sem(RB + n1(p, j)), dev).start()
            if p == 0:
                pltpu.make_async_copy(tab.at[j, me], tabr.at[j, me], sem(2 * RB + nt(j))).start()
            pltpu.make_async_copy(src, ag[j].at[p, me], sem(2 * RB + n1(p, j))).start()

    def wait1(p, j):
        if p == 0:
            dummy = tabr.at[j, pl.ds(0, 3)]
            done = remote(dummy, dummy, sem(nt(j)), sem(RB + nt(j)), device(pos, other))
            done.wait_recv()
            done.wait_send()
            pltpu.make_async_copy(tab.at[j, 0], tabr.at[j, 0], sem(2 * RB + nt(j))).wait()
        dummy = ag[j].at[p, pl.ds(0, 3)]
        done = remote(dummy, dummy, sem(n1(p, j)), sem(RB + n1(p, j)), device(pos, other))
        done.wait_recv()
        done.wait_send()
        dummy = ag[j].at[p, 0]
        pltpu.make_async_copy(dummy, dummy, sem(2 * RB + n1(p, j))).wait()

    sub3 = lax.broadcasted_iota(jnp.int32, (32, 8, 128), 1).astype(F32)

    def build_masks(j):
        wt_acc = jnp.zeros((32, 8, 1), F32)
        for a in range(4):
            code = tabr[j, a, 0].reshape(32, 1, 128)
            wgt = tabr[j, a, 1].reshape(32, 1, 128)
            code = jnp.broadcast_to(code, (32, 8, 128))
            wgt = jnp.broadcast_to(wgt, (32, 8, 128))
            hit = jnp.where(code == sub3, 1.0, 0.0)
            pm[j, a] = hit.reshape(256, 128).astype(BF16)
            wmain[j, a] = jnp.sum(hit * wgt, axis=2, keepdims=True).reshape(256, 1)
            for h in range(2):
                mine = jnp.where((code == 8.0) & (sub3 == float(h * 4 + a)), 1.0, 0.0)
                pm[j, 4 + h * 4 + a] = mine.reshape(256, 128).astype(BF16)
                wt_acc = wt_acc + jnp.sum(mine * wgt, axis=2, keepdims=True)
        wtail[j] = wt_acc.reshape(256, 1)

    def pack(p, j):
        half = WID[j] // 2

        def per_block(a, carry):
            for s, n in cols(j):
                res = jnp.dot(pm[j, a], ag[j][p, a, :, s : s + n], preferred_element_type=F32)
                if p == 0:
                    res = res * wmain[j, a]
                send2[j][p, :, :, a, :, s : s + n] = res.reshape(4, 8, 8, n).astype(BF16)
            return carry

        lax.fori_loop(0, 4, per_block, 0)
        for s in range(0, half, 128):
            res = jnp.zeros((256, 128), F32)
            for h in range(2):
                for a in range(4):
                    s0 = h * half + s
                    res = res + jnp.dot(
                        pm[j, 4 + h * 4 + a], ag[j][p, a, :, s0 : s0 + 128], preferred_element_type=F32
                    )
            if p == 0:
                res = res * wtail[j]
            send2t[j][p, :, :, :, s : s + 128] = res.reshape(4, 8, 8, 128).astype(BF16)

    def stage2(p, j):
        rb = ROLES[j][1]
        me = pos[rb]
        for d in (1, 2, 3):
            to = lax.rem(me + d, 4)
            dev = device(moved(pos, rb, d), core)
            remote(send2[j].at[p, to], recv2[j].at[p, me], sem(n2(p, j, 0)), sem(RB + n2(p, j, 0)), dev).start()
            remote(send2t[j].at[p, to], recv2t[j].at[p, me], sem(n2(p, j, 1)), sem(RB + n2(p, j, 1)), dev).start()

    def wait2(p, j):
        for t, ref in ((0, recv2), (1, recv2t)):
            dummy = ref[j].at[p, pl.ds(0, 3)]
            done = remote(dummy, dummy, sem(n2(p, j, t)), sem(RB + n2(p, j, t)), device(pos, other))
            done.wait_recv()
            done.wait_send()

    def stage3(p, j):
        ra, rb, rc = ROLES[j]
        for d in (0, 1, 2, 3):
            dst_pos = moved(pos, rc, d)
            for flip in (0, 1):
                k = core if flip == 0 else other
                ck = dst_pos[rc] * 2 + k
                for q in range(4):
                    b = lax.rem(pos[rb] + q, 4)
                    src = (send2 if q == 0 else recv2)[j].at[p, b, ck]
                    srct = (send2t if q == 0 else recv2t)[j].at[p, b, ck]
                    dst = main_at(mains[p], j, b, pos[rc], core)
                    dstt = tails[p][j].at[pos[rc] * 2 + core, b]
                    if d == 0 and flip == 0:
                        pltpu.make_async_copy(src, dst, sem(2 * RB + n3(p, j, 0))).start()
                        pltpu.make_async_copy(srct, dstt, sem(2 * RB + n3(p, j, 1))).start()
                    else:
                        dev = device(dst_pos, k)
                        remote(src, dst, sem(n3(p, j, 0)), sem(RB + n3(p, j, 0)), dev).start()
                        remote(srct, dstt, sem(n3(p, j, 1)), sem(RB + n3(p, j, 1)), dev).start()

    def wait3(p, j):
        for t, ref in ((0, send2), (1, send2t)):
            dummy = ref[j].at[p, :, pl.ds(0, 7)]
            done = remote(dummy, dummy, sem(n3(p, j, t)), sem(RB + n3(p, j, t)), device(pos, other))
            done.wait_recv()
            done.wait_send()
            dummy = ref[j].at[p, :, 0]
            pltpu.make_async_copy(dummy, dummy, sem(2 * RB + n3(p, j, t))).wait()

    stage1(0)
    stage1(1)
    for j in range(3):
        wait1(0, j)
        build_masks(j)
        pack(0, j)
        stage2(0, j)
    for j in range(3):
        wait1(1, j)
        pack(1, j)
    keep = pltpu.make_async_copy(pm, masks, sem(3 * RB))
    keep.start()
    for j in range(3):
        wait2(0, j)
        stage3(0, j)
    for j in range(3):
        stage2(1, j)
    for j in range(3):
        wait2(1, j)
        stage3(1, j)
    for p in range(2):
        for j in range(3):
            wait3(p, j)
    keep.wait()


def dispatch(ids_t, w_t, grad, rows):
    any_spec = pl.BlockSpec(memory_space=pl.ANY)
    vmem = pl.BlockSpec(memory_space=pltpu.VMEM)
    shape = jax.ShapeDtypeStruct
    main = shape((4, 4, 4, 2, 8, 4096), BF16)
    tails = [shape((8, 4, 8, w // 2), BF16) for w in WID]
    scratch = [pltpu.VMEM((2, 4, 128, w), BF16) for w in WID]
    scratch += [pltpu.VMEM((2, 4, 8, 4, 8, w), BF16) for w in WID] * 2
    scratch += [pltpu.VMEM((2, 4, 8, 8, w // 2), BF16) for w in WID] * 2
    scratch += [
        pltpu.VMEM((3, 4, 2, 32, 128), F32),
        pltpu.VMEM((3, 4, 2, 32, 128), F32),
        pltpu.VMEM((3, 12, 256, 128), BF16),
        pltpu.VMEM((3, 4, 256, 1), F32),
        pltpu.VMEM((3, 256, 1), F32),
        pltpu.SemaphoreType.DMA((100,)),
    ]
    return pl.pallas_call(
        dispatch_kernel,
        out_shape=[main, main] + tails + tails + [shape((3, 12, 256, 128), BF16)],
        in_specs=[vmem] * 4,
        out_specs=[any_spec] * 9,
        scratch_shapes=scratch,
        compiler_params=pltpu.CompilerParams(
            collective_id=0, has_side_effects=True, vmem_limit_bytes=62 << 20
        ),
        name="dispatch",
    )(ids_t, w_t, grad, rows)


def combine_kernel(*refs):
    main, t0, t1, t2, masks, out = refs[:6]
    tails = (t0, t1, t2)
    scratch = refs[6:]
    r1 = scratch[0:3]
    r2 = scratch[3:6]
    r1t = scratch[6:9]
    r2t = scratch[9:12]
    part = scratch[12:15]
    got = scratch[15:18]
    own = scratch[18]
    sems = scratch[19]
    pos, core = coords()
    other = 1 - core
    barrier, count = greet(pos, core)
    pl.semaphore_wait(barrier, count)
    RB = 15

    def sem(i):
        return sems.at[i]

    def n1(j, t):
        return j * 2 + t

    def n2(j, t):
        return 6 + j * 2 + t

    def n3(j):
        return 12 + j

    def stage1(j):
        ra, rb, rc = ROLES[j]
        mine = pos[rc] * 2 + core
        for d in (0, 1, 2, 3):
            dst_pos = moved(pos, rc, d)
            for flip in (0, 1):
                k = core if flip == 0 else other
                ck = dst_pos[rc] * 2 + k
                for b in range(4):
                    src = main_at(main, j, b, dst_pos[rc], k)
                    dst = r1[j].at[b, mine]
                    if d == 0 and flip == 0:
                        pltpu.make_async_copy(src, dst, sem(2 * RB + n1(j, 0))).start()
                    else:
                        remote(src, dst, sem(n1(j, 0)), sem(RB + n1(j, 0)), device(dst_pos, k)).start()
                src = tails[j].at[ck]
                dst = r1t[j].at[:, mine]
                if d == 0 and flip == 0:
                    pltpu.make_async_copy(src, dst, sem(2 * RB + n1(j, 1))).start()
                else:
                    remote(src, dst, sem(n1(j, 1)), sem(RB + n1(j, 1)), device(dst_pos, k)).start()

    def wait1(j):
        for t, ref in ((0, r1), (1, r1t)):
            dummy = ref[j].at[:, pl.ds(0, 7)]
            done = remote(dummy, dummy, sem(n1(j, t)), sem(RB + n1(j, t)), device(pos, other))
            done.wait_recv()
            done.wait_send()
            dummy = ref[j].at[:, 0]
            pltpu.make_async_copy(dummy, dummy, sem(2 * RB + n1(j, t))).wait()

    def stage2(j):
        rb = ROLES[j][1]
        me = pos[rb]
        for t, (a, b) in enumerate(((r1, r2), (r1t, r2t))):
            for d in (1, 2, 3):
                to = lax.rem(me + d, 4)
                dev = device(moved(pos, rb, d), core)
                remote(a[j].at[to], b[j].at[me], sem(n2(j, t)), sem(RB + n2(j, t)), dev).start()
            pltpu.make_async_copy(a[j].at[me], b[j].at[me], sem(2 * RB + n2(j, t))).start()

    def wait2(j):
        for t, ref in ((0, r2), (1, r2t)):
            dummy = ref[j].at[pl.ds(0, 3)]
            done = remote(dummy, dummy, sem(n2(j, t)), sem(RB + n2(j, t)), device(pos, other))
            done.wait_recv()
            done.wait_send()
            dummy = ref[j].at[0]
            pltpu.make_async_copy(dummy, dummy, sem(2 * RB + n2(j, t))).wait()

    def fold(j):
        ra = ROLES[j][0]
        half = WID[j] // 2
        for d in range(4):
            a = lax.rem(pos[ra] + d, 4)
            mt = masks[j, a]
            for s in range(0, half, 128):
                tail = r2t[j][:, :, :, s : s + 128].astype(F32).reshape(256, 128).astype(BF16)
                for h in range(2):
                    s0 = h * half + s
                    rows = r2[j][:, :, a, :, s0 : s0 + 128].astype(F32).reshape(256, 128).astype(BF16)
                    res = lax.dot_general(mt, rows, (((0,), (0,)), ((), ())), preferred_element_type=F32)
                    res = res + lax.dot_general(
                        masks[j, 4 + h * 4 + a], tail, (((0,), (0,)), ((), ())), preferred_element_type=F32
                    )
                    if d == 0:
                        own[:, OFF[j] + s0 : OFF[j] + s0 + 128] = res
                    else:
                        part[j][d - 1, :, s0 : s0 + 128] = res.astype(BF16)

    def stage3(j):
        ra = ROLES[j][0]
        for d in (1, 2, 3):
            dev = device(moved(pos, ra, d), core)
            remote(part[j].at[d - 1], got[j].at[d - 1], sem(n3(j)), sem(RB + n3(j)), dev).start()

    def finish(j):
        dummy = got[j]
        done = remote(dummy, dummy, sem(n3(j)), sem(RB + n3(j)), device(pos, other))
        done.wait_recv()
        done.wait_send()
        for s, n in cols(j):
            total = own[:, OFF[j] + s : OFF[j] + s + n]
            for d in range(3):
                total = total + got[j][d, :, s : s + n].astype(F32)
            out[:, OFF[j] + s : OFF[j] + s + n] = total.astype(BF16)

    for j in range(3):
        stage1(j)
    for j in range(3):
        wait1(j)
        stage2(j)
    for j in range(3):
        wait2(j)
        fold(j)
        stage3(j)
    for j in range(3):
        finish(j)


def combine(main, tails, masks):
    any_spec = pl.BlockSpec(memory_space=pl.ANY)
    vmem = pl.BlockSpec(memory_space=pltpu.VMEM)
    scratch = [pltpu.VMEM((4, 8, 4, 8, w), BF16) for w in WID] * 2
    scratch += [pltpu.VMEM((4, 8, 8, w // 2), BF16) for w in WID] * 2
    scratch += [pltpu.VMEM((3, 128, w), BF16) for w in WID] * 2
    scratch += [pltpu.VMEM((128, 4096), F32), pltpu.SemaphoreType.DMA((45,))]
    return pl.pallas_call(
        combine_kernel,
        out_shape=jax.ShapeDtypeStruct((128, 4096), BF16),
        in_specs=[any_spec] * 4 + [vmem],
        out_specs=vmem,
        scratch_shapes=scratch,
        compiler_params=pltpu.CompilerParams(
            collective_id=1, has_side_effects=True, vmem_limit_bytes=62 << 20
        ),
        name="combine",
    )(main, *tails, masks)


def tail_rows(j):
    i = jnp.arange(256, dtype=jnp.int32)
    ra, rb, rc = ROLES[j]
    v = [None] * 3
    v[rc] = i // 64
    v[rb] = (i // 8) % 4
    v[ra] = i % 4
    block = ((v[0] * 4 + v[1]) * 4 + v[2]) * 2 + (i // 32) % 2
    half = (i // 4) % 2
    return block, half


def unpack_tails(tails):
    parts = []
    blocks = jnp.arange(128, dtype=jnp.int32)
    for j in range(3):
        block, half = tail_rows(j)
        flat = tails[j].reshape(256, WID[j] // 2)
        for h in range(2):
            pick = ((blocks[:, None] == block[None, :]) & (half[None, :] == h)).astype(BF16)
            parts.append(jnp.dot(pick, flat, preferred_element_type=F32).astype(BF16))
    return jnp.concatenate(parts, axis=1)


def pack_tails(tail):
    packed = []
    blocks = jnp.arange(128, dtype=jnp.int32)
    for j in range(3):
        block, half = tail_rows(j)
        w = WID[j] // 2
        same = block[:, None] == blocks[None, :]
        picks = [(same & (half[:, None] == h)).astype(BF16) for h in range(2)]
        lo = tail[:, OFF[j] : OFF[j] + w]
        hi = tail[:, OFF[j] + w : OFF[j] + 2 * w]
        res = jnp.dot(picks[0], lo, preferred_element_type=F32) + jnp.dot(
            picks[1], hi, preferred_element_type=F32
        )
        packed.append(res.astype(BF16).reshape(8, 4, 8, w))
    return packed


def canonical_slots():
    i = jnp.arange(1152, dtype=jnp.int32)
    is_tail = i >= 1024
    block = jnp.where(is_tail, i - 1024, i // 8)
    r = jnp.where(is_tail, 8, i % 8)
    x, y, z, k = block // 32, (block // 8) % 4, (block // 2) % 4, block % 2
    b = ((y * 2 + z % 2) * 4 + x) * 4 + (z // 2) * 2 + k
    return b * 9 + r


def mm(a, b, da, db):
    return lax.dot_general(a, b, (((da,), (db,)), ((), ())), preferred_element_type=F32)


def expert_backward(parts_g, parts_x, pre, wg, wu, wd, ga, go, ua, uo, da, do):
    outs = []
    sums = [0.0] * 5
    both_in = jnp.concatenate([ga, ua], axis=0)
    for g, x, (gate_pre, up_pre) in zip(parts_g, parts_x, pre):
        gate = gate_pre.astype(F32)
        up = up_pre.astype(F32)
        sig = jax.nn.sigmoid(gate)
        silu = gate * sig
        hidden = (silu * up).astype(BF16)
        down_lora = mm(hidden, da, 1, 1).astype(BF16)
        grad_lora = mm(g, do, 1, 1).astype(BF16)
        sums[0] = sums[0] + mm(down_lora, g, 0, 0)
        sums[1] = sums[1] + mm(grad_lora, hidden, 0, 0)
        gh = mm(g, wd, 1, 1) + adapter_scale * mm(grad_lora, da, 1, 0)
        gg = (gh * up * sig * (1.0 + gate * (1.0 - sig))).astype(BF16)
        gu = (gh * silu).astype(BF16)
        deltas = mm(x, both_in, 1, 1).astype(BF16)
        sums[2] = sums[2] + mm(deltas[:, :16], gg, 0, 0)
        sums[3] = sums[3] + mm(deltas[:, 16:], gu, 0, 0)
        back = jnp.concatenate([mm(gg, go, 1, 1).astype(BF16), mm(gu, uo, 1, 1).astype(BF16)], axis=1)
        sums[4] = sums[4] + mm(back, x, 0, 0)
        left = jnp.concatenate([gg, gu, back], axis=1)
        right = jnp.concatenate([wg, wu, (both_in.astype(F32) * adapter_scale).astype(BF16).T], axis=1)
        outs.append(mm(left, right, 1, 1).astype(BF16))
    r = [(adapter_scale * s).astype(BF16) for s in sums]
    return outs, (r[4][:16], r[2], r[4][16:], r[3], r[1], r[0])


def local(rows, grad, choice, weight, wg, wu, wd, ga, go, ua, uo, da, do, gate_pre, up_pre):
    res = dispatch(choice.T, weight.T, grad, rows)
    gmain, xmain = res[0].reshape(1024, 4096), res[1].reshape(1024, 4096)
    gtail, xtail = unpack_tails(res[2:5]), unpack_tails(res[5:8])
    masks = res[8]
    order = (canonical_slots()[:, None] == jnp.arange(1152, dtype=jnp.int32)[None, :]).astype(BF16)
    gp = jnp.dot(order, gate_pre[0], preferred_element_type=F32).astype(BF16)
    up = jnp.dot(order, up_pre[0], preferred_element_type=F32).astype(BF16)
    outs, grads = expert_backward(
        (gmain, gtail),
        (xmain, xtail),
        ((gp[:1024], up[:1024]), (gp[1024:], up[1024:])),
        wg[0], wu[0], wd[0], ga[0], go[0], ua[0], uo[0], da[0], do[0],
    )
    grad_in = combine(outs[0].reshape(4, 4, 4, 2, 8, 4096), pack_tails(outs[1]), masks)
    return (grad_in,) + tuple(v[None] for v in grads)


def solution(mesh):
    row = P(("ctx", "ep"), None)
    cube = P(("ctx", "ep"), None, None)
    return jax.shard_map(
        local,
        mesh=mesh,
        in_specs=(row,) * 4 + (cube,) * 11,
        out_specs=(row,) + (cube,) * 6,
        check_vma=False,
    )
```

time: 804 us -> 421 us (0.52)
  the two profiles are of different devices: /device:TPU:12 before, /device:TPU:1 now
where the time goes in v1:
time: 421 us; the launch traced here: 415 us
  Pallas kernels  302 us (72%)
  matrix products  105 us (25%)
  local copies, waits for them, and re-layouts  5.44 us (1%)
    pallas_call x1, Pallas kernels, dispatch(): pl.pallas_call(dispatch_kernel, out_shape=[main, main] + tails + tails +...  192 us
    pallas_call x1, Pallas kernels, combine(): pl.pallas_call(combine_kernel, out_shape=jax.ShapeDtypeStruct((128, 4096)...  110 us
    dot_general x24, matrix products, mm(): lax.dot_general(a, b, (((da,), (db,)), ((), ())), preferred_element_type=...  72.1 us
    dot_general x1, matrix products, local(): gp = jnp.dot(order, gate_pre[0], preferred_element_type=F32).astype(BF16)  15.5 us
    dot_general x12, matrix products, unpack_tails(): parts.append(jnp.dot(pick, flat, preferred_element_type=F32).astype(BF16))  10.4 us

profile of v1, /device:TPU:1, one launch (start us, length us, event | category | flops | bytes accessed | tf_op | source)
XLA Modules:
  0.0 415.2 jit_solution(6287224234666004918)
XLA Ops:
  0.7 192.1 %dispatch.1 = (bf16[4,4,4,2,8,4096]{5,4,3,2,1,0:T(8,128)(2,1)}, bf16[4,4,4,2,8,4096]{5,4,3,2,1,0:T(8,128)(2,1)}, bf16[8,4,8,640]{3,2,1,0:T(8,128)(2,1)}, bf16[8,...) custom-call(s32[8,128]{1,0:T(8,128)} %bitcast.146, ...), custom_call_target="tpu_custom_call" | custom-call | tf_op jit(solution)/shard_map/dispatch/pallas_call | solution.py:298
  194.0 1.2 fusion.51
  195.2 1.2 fusion.50
  196.4 1.2 fusion.49
  197.7 1.2 fusion.43
  198.9 1.2 fusion.42
  200.1 4.6 %fusion = f32[128,768]{0,1:T(8,128)S(1)} fusion(bf16[128,4096]{1,0:T(8,128)(2,1)S(1)} %fusion.42, bf16[1,768,4096]{2,1,0:T(8,128)(2,1)} %param.21), kind=kOutput, calls=%fused_computation.2 | convolution fusion | flops 805306368 | bytes 7733248 | tf_op jit(solution)/shard_map/dot_general | solution.py:513
  205.2 2.8 fusion.13
  208.1 15.5 %fusion.14 = bf16[1152,768]{0,1:T(8,128)(2,1)S(1)} fusion(s32[1152]{0:T(1024)S(1)} %fusion.182, bf16[1,1152,768]{2,1,0:T(8,128)(2,1)S(1)} %copy-done.21), kind=kOutput, calls=%fused_computation.24 | convolution fusion | flops 2040643584 | bytes 3543552 | tf_op jit(solution)/shard_map/dot_general | solution.py:551
  223.6 1.2 fusion.72
  224.9 2.3 convolution_convert_fusion.18
  227.8 9.5 %fusion.24 = (bf16[1024,768]{0,1:T(8,128)(2,1)S(1)}, bf16[1024,768]{0,1:T(8,128)(2,1)}, bf16[1024,768]{0,1:T(8,128)(2,1)}) fusion(bf16[1152,768]{0,1:T(8,128)(2,1)S(1)} %fusion.14, bf16[1152,768]{0,1:T(8,128)(2,1)S(1)} %fusion.13, f32[1024,768]{0,1:T(8,128)S(1)} %fusion.172, bf16[1024,4096]{1,0:T(8,128)(2,1)S(1)} %bitcast.121, ...), kind=kOutput, calls=%fused_computation.34 | convolution fusion | flops 6457393152 | bytes 25690112 | tf_op jit(solution)/shard_map/dot_general | solution.py:513
  237.3 7.0 %fusion.44 = f32[16,4096]{1,0:T(8,128)} fusion(bf16[1024,4096]{1,0:T(8,128)(2,1)} %bitcast.117, bf16[1024,768]{0,1:T(8,128)(2,1)} %get-tuple-element.29, bf16[1,16,768]{2,1,0:T(8,128)(2,1)S(1)} %copy-done.11), kind=kOutput, calls=%fused_computation.63 | convolution fusion | flops 159399936 | bytes 10248192 | tf_op jit(solution)/shard_map/dot_general | solution.py:513
  244.3 2.4 fusion.12
  246.7 1.9 fusion.226
  248.7 1.7 fusion.59
  251.6 1.2 fusion.47
  254.3 6.1 %convolution_convert_fusion.14 = bf16[1024,32]{0,1:T(8,128)(2,1)S(1)} fusion(bf16[1024,4096]{1,0:T(8,128)(2,1)} %bitcast.113, bf16[16,4096]{1,0:T(8,128)(2,1)S(1)} %bitcast.141, bf16[16,4096]{1,0:T(8,128)(2,1)S(1)} %bitcast.144), kind=kOutput, calls=%fused_computation.80 | convolution fusion | flops 268992512 | bytes 8716288 | tf_op jit(solution)/shard_map/dot_general | solution.py:513
  264.1 1.5 fusion.119
  267.4 2.3 copy.22
  269.6 7.8 %fusion.7 = bf16[128,4096]{1,0:T(8,128)(2,1)S(1)} fusion(bf16[4096,32]{1,0:T(8,128)(2,1)} %copy.22, bf16[4096,768]{1,0:T(8,128)(2,1)} %bitcast.148, bf16[4096,768]{1,0:T(8,128)(2,1)} %bitcast.150, bf16[128,16]{0,1:T(8,128)(2,1)} %copy-done.19, bf16[128,16]{0,1:T(8,128)(2,1)} %copy-done.20, bf16[128,768]{0,1:T(8,128)(2,1)} %get-tuple-element.30, ...), kind=kOutput, calls=%fused_computation.10 | convolution fusion | flops 1684832256 | bytes 14295040 | tf_op jit(solution)/shard_map/dot_general | solution.py:513
  281.5 20.7 %convolution_convert_fusion = bf16[1024,4096]{1,0:T(8,128)(2,1)} fusion(bf16[4096,32]{1,0:T(8,128)(2,1)S(1)} %copy-done.7, bf16[4096,768]{1,0:T(8,128)(2,1)} %bitcast.149, bf16[4096,768]{1,0:T(8,128)(2,1)} %bitcast.151, bf16[1024,16]{0,1:T(8,128)(2,1)S(1)} %convolution_convert_fusion.15, bf16[1024,16]{0,1:T(8,128)(2,1)S(1)} %convolution_convert_fusion.16, ...), kind=kOutput, calls=%fused_computation.1 | convolution fusion | flops 13208911872 | bytes 24444928 | tf_op jit(solution)/shard_map/dot_general | solution.py:513
  302.2 110.2 %combine.1 = bf16[128,4096]{1,0:T(8,128)(2,1)} custom-call(bf16[4,4,4,2,8,4096]{5,4,3,2,1,0:T(8,128)(2,1)} %bitcast.122, bf16[8,4,8,640]{3,2,1,0:T(8,128)(2,1)} %bitcast.131, bf16[8,4,8,640]{3,2,1,0:T(8,128)(2,1)} %bitcast.130, bf16[8,4,8,768]{3,2,1,0:T(8,128)(2,1)} %bitcast.125, bf16[3,12,256,128]{3,2,1,0:T(8,128)(2,1)} %get-tuple-element.20.refs_4_), custom_call_target="tpu_custom_call" | custom-call | tf_op jit(solution)/shard_map/combine/pallas_call | solution.py:448
  412.5 2.3 copy.38
  (91 shorter events, 14.3 us)
Async XLA Ops:
  0.6 204.5 %copy-start = (bf16[1,1152,768]{2,1,0:T(8,128)(2,1)S(1)}, bf16[1,1152,768]{2,1,0:T(8,128)(2,1)}, u32[]{:S(2)}) copy-start(bf16[1,1152,768]{2,1,0:T(8,128)(2,1)} %param.29) | copy-start | bytes 5308420
  197.6 7.1 %copy-start.14 = (s32[256]{0:T(256)}, s32[256]{0:T(256)S(1)}, u32[]{:S(2)}) copy-start(s32[256]{0:T(256)S(1)} %multiply_add_fusion.1) | copy-start | bytes 3076
  200.1 4.6 %copy-start.10 = (bf16[1,16,4096]{2,1,0:T(8,128)(2,1)S(1)}, bf16[1,16,4096]{2,1,0:T(8,128)(2,1)}, u32[]{:S(2)}) copy-start(bf16[1,16,4096]{2,1,0:T(8,128)(2,1)} %param.27) | copy-start | bytes 393220
  205.1 18.5 %copy-start.17 = (bf16[128,16]{0,1:T(8,128)(2,1)}, bf16[128,16]{0,1:T(8,128)(2,1)S(1)}, u32[]{:S(2)}) copy-start(bf16[128,16]{0,1:T(8,128)(2,1)S(1)} %convolution_convert_fusion.22) | copy-start | bytes 12292
  205.2 2.9 copy-start.21
  205.2 19.7 %slice-start.2 = ((s8[8388608]{0:T(1024)(128)(4,1)}), s8[4194304]{0:T(1024)(128)(4,1)S(1)}, s32[]{:S(2)}) async-start(s8[8388608]{0:T(1024)(128)(4,1)} %bitcast.118), calls=%async_computation.2 | async-start | bytes 8388608
  208.1 15.6 %copy-start.11 = (bf16[1,16,768]{2,1,0:T(8,128)(2,1)S(1)}, bf16[1,16,768]{2,1,0:T(8,128)(2,1)}, u32[]{:S(2)}) copy-start(bf16[1,16,768]{2,1,0:T(8,128)(2,1)} %param.26) | copy-start | bytes 73732
  208.1 16.8 %slice-start.3 = ((s8[8388608]{0:T(1024)(128)(4,1)}), s8[4194304]{0:T(1024)(128)(4,1)S(1)}, s32[]{:S(2)}) async-start(s8[8388608]{0:T(1024)(128)(4,1)} %bitcast.118), calls=%async_computation.3 | async-start | bytes 8388608
  223.6 4.2 slice-start.4
  224.9 2.9 slice-start.5
  244.3 4.3 %copy-start.18 = (bf16[128,16]{0,1:T(8,128)(2,1)S(1)}, bf16[128,16]{0,1:T(8,128)(2,1)}, u32[]{:S(2)}) copy-start(bf16[128,16]{0,1:T(8,128)(2,1)} %copy-done.17) | copy-start | bytes 12292
  244.3 8.5 %copy-start.4 = (bf16[8,4,8,640]{3,2,1,0:T(8,128)(2,1)S(1)}, bf16[8,4,8,640]{3,2,1,0:T(8,128)(2,1)}, u32[]{:S(2)}) copy-start(bf16[8,4,8,640]{3,2,1,0:T(8,128)(2,1)} %get-tuple-element.23) | copy-start | bytes 983044
  244.3 9.0 %copy-start.3 = (bf16[8,4,8,768]{3,2,1,0:T(8,128)(2,1)S(1)}, bf16[8,4,8,768]{3,2,1,0:T(8,128)(2,1)}, u32[]{:S(2)}) copy-start(bf16[8,4,8,768]{3,2,1,0:T(8,128)(2,1)} %get-tuple-element.24) | copy-start | bytes 1179652
  244.3 9.0 %copy-start.15 = (s32[256]{0:T(256)S(1)}, s32[256]{0:T(256)}, u32[]{:S(2)}) copy-start(s32[256]{0:T(256)} %copy-done.14) | copy-start | bytes 3076
  244.3 9.4 %copy-start.5 = (bf16[1,16,4096]{2,1,0:T(8,128)(2,1)S(1)}, bf16[1,16,4096]{2,1,0:T(8,128)(2,1)}, u32[]{:S(2)}) copy-start(bf16[1,16,4096]{2,1,0:T(8,128)(2,1)} %param.24) | copy-start | bytes 393220
  246.7 7.0 %copy-start.6 = (bf16[1,16,4096]{2,1,0:T(8,128)(2,1)S(1)}, bf16[1,16,4096]{2,1,0:T(8,128)(2,1)}, u32[]{:S(2)}) copy-start(bf16[1,16,4096]{2,1,0:T(8,128)(2,1)} %param.22) | copy-start | bytes 393220
  253.8 6.7 %copy-start.2 = (bf16[1024,768]{0,1:T(8,128)(2,1)S(1)}, bf16[1024,768]{0,1:T(8,128)(2,1)}, u32[]{:S(2)}) copy-start(bf16[1024,768]{0,1:T(8,128)(2,1)} %get-tuple-element.26) | copy-start | bytes 4718596
  254.2 9.8 %slice-start = ((s8[8388608]{0:T(1024)(128)(4,1)}), s8[4194304]{0:T(1024)(128)(4,1)S(1)}, s32[]{:S(2)}) async-start(s8[8388608]{0:T(1024)(128)(4,1)} %bitcast.114), calls=%async_computation | async-start | bytes 8388608
  254.2 6.7 %copy-start.9 = (bf16[128,768]{0,1:T(8,128)(2,1)S(1)}, bf16[128,768]{0,1:T(8,128)(2,1)}, u32[]{:S(2)}) copy-start(bf16[128,768]{0,1:T(8,128)(2,1)} %get-tuple-element.30) | copy-start | bytes 589828
  254.2 9.8 %slice-start.1 = ((s8[8388608]{0:T(1024)(128)(4,1)}), s8[4194304]{0:T(1024)(128)(4,1)S(1)}, s32[]{:S(2)}) async-start(s8[8388608]{0:T(1024)(128)(4,1)} %bitcast.114), calls=%async_computation.1 | async-start | bytes 8388608
  260.4 2.8 copy-start.13
  269.6 7.8 %copy-start.16 = (s32[256]{0:T(256)S(1)}, s32[256]{0:T(256)}, u32[]{:S(2)}) copy-start(s32[256]{0:T(256)} %copy-done.14) | copy-start | bytes 3076
  277.4 4.1 copy-start.7
  302.2 112.5 %copy-start.1 = (bf16[1,1152,768]{2,1,0:T(8,128)(2,1)S(1)}, bf16[1,1152,768]{2,1,0:T(8,128)(2,1)}, u32[]{:S(2)}) copy-start(bf16[1,1152,768]{2,1,0:T(8,128)(2,1)} %param.29) | copy-start | bytes 5308420
  (4 other events, 9.1 us)

commit v2 on v1

v2 whole, which is shorter than its diff:
```python
import jax
import jax.numpy as jnp
from jax import lax
from jax.experimental import pallas as pl
from jax.experimental.pallas import tpu as pltpu
from jax.sharding import PartitionSpec as P

MESH = pl.DeviceIdType.MESH
ROLES = ((0, 1, 2), (1, 2, 0), (2, 0, 1))
WID = (1280, 1280, 1536)
OFF = (0, 1280, 2560)
CHUNK = 256
F32 = jnp.float32
BF16 = jnp.bfloat16
adapter_scale = 2.0


def coords():
    c = lax.axis_index("ctx")
    e = lax.axis_index("ep")
    x = lax.rem(c, 4)
    y = c // 8
    z = (e // 2) * 2 + lax.rem(c // 4, 2)
    return (x, y, z), lax.rem(e, 2)


def device(pos, core):
    x, y, z = pos
    return ((y * 2 + lax.rem(z, 2)) * 4 + x, (z // 2) * 2 + core)


def moved(pos, axis, d):
    out = list(pos)
    out[axis] = lax.rem(pos[axis] + d, 4)
    return tuple(out)


def greet(pos, core):
    barrier = pltpu.get_barrier_semaphore()
    other = 1 - core
    peers = [device(pos, other)]
    for axis in range(3):
        for d in (1, 2, 3):
            peers.append(device(moved(pos, axis, d), core))
            peers.append(device(moved(pos, axis, d), other))
    for peer in peers:
        pl.semaphore_signal(barrier, inc=1, device_id=peer, device_id_type=MESH)
    return barrier, len(peers)


def remote(src, dst, ssem, rsem, dev):
    return pltpu.make_async_remote_copy(
        src_ref=src, dst_ref=dst, send_sem=ssem, recv_sem=rsem, device_id=dev, device_id_type=MESH
    )


def expert_ids(j, shape):
    i = lax.broadcasted_iota(jnp.int32, shape, 0)
    v = [None] * 3
    a, b, c = ROLES[j]
    v[a] = i // 32
    v[b] = (i // 8) % 4
    v[c] = (i // 2) % 4
    k = i % 2
    x, y, z = v
    return ((y * 2 + z % 2) * 4 + x) * 4 + (z // 2) * 2 + k


def main_at(ref, j, b, c, k):
    ra, rb, rc = ROLES[j]
    idx = [None] * 3
    idx[ra] = slice(None)
    idx[rb] = b
    idx[rc] = c
    return ref.at[idx[0], idx[1], idx[2], k, :, pl.ds(OFF[j], WID[j])]


def cols(j):
    return [(s, CHUNK) for s in range(0, WID[j], CHUNK)]


def rows_of(i):
    out = []
    for j in range(3):
        ra, rb, rc = ROLES[j]
        v = [None] * 3
        v[rc] = i // 64
        v[rb] = (i // 8) % 4
        v[ra] = i % 4
        out.append((((v[0] * 4 + v[1]) * 4 + v[2]) * 2 + (i // 32) % 2, (i // 4) % 2))
    return out


def slot_of(block, r):
    x, y, z, k = block // 32, (block // 8) % 4, (block // 2) % 4, block % 2
    return (((y * 2 + z % 2) * 4 + x) * 4 + (z // 2) * 2 + k) * 9 + r


def mm(a, b, da, db):
    return lax.dot_general(a, b, (((da,), (db,)), ((), ())), preferred_element_type=F32)


def flat(v):
    n = v.shape[-1]
    return v.astype(F32).reshape(-1, n).astype(BF16)


N_IN = 15
N_OUT = 7
N_TMP = 27


def block_kernel(*refs):
    (ids_ref, wt_ref, g_hbm, x_hbm, gate_hbm, up_hbm, wg_hbm, wu_hbm, wd_hbm, ga, go, ua, uo, da, do) = refs[:N_IN]
    out, o_gi, o_go, o_ui, o_uo, o_di, o_do = refs[N_IN : N_IN + N_OUT]
    tmp = refs[N_IN + N_OUT : N_IN + N_OUT + N_TMP]
    gmain, xmain, rmain = tmp[0:3]
    tails = (tmp[3:6], tmp[6:9])
    rtails = tmp[9:12]
    recv2, recv2t = tmp[12:15], tmp[15:18]
    r1, r1t = tmp[18:21], tmp[21:24]
    r2t_hbm = tmp[24:27]
    sc = refs[N_IN + N_OUT + N_TMP :]
    ag, send2, send2t, r2, got = sc[0:3], sc[3:6], sc[6:9], sc[9:12], sc[12:15]
    (tab, tabr, pm, wmain, wtail, own, gg, gu, gtail, dlora, back, acc_do, acc_di, acc_in, acc_o, wide, narrow, sems, rsems, lsems) = sc[15:]
    mains = (gmain, xmain)
    data = (g_hbm, x_hbm)
    pos, core = coords()
    other = 1 - core
    barrier, count = greet(pos, core)

    row = lax.broadcasted_iota(jnp.int32, (128, 128), 0)
    lane = lax.broadcasted_iota(jnp.int32, (128, 128), 1)
    strict = (row < lane).astype(BF16)
    for j in range(3):
        eid = expert_ids(j, (128, 128))
        hit = jnp.zeros((128, 128), F32)
        wgt = jnp.zeros((128, 128), F32)
        for k in range(8):
            same = eid == ids_ref[k : k + 1, :]
            hit = hit + jnp.where(same, 1.0, 0.0)
            wgt = wgt + jnp.where(same, wt_ref[k : k + 1, :], 0.0)
        rank = jnp.dot(hit.astype(BF16), strict, preferred_element_type=F32)
        code = jnp.where(hit > 0.5, rank, -1.0)
        tab[j, :, 0] = code.reshape(4, 32, 128)
        tab[j, :, 1] = wgt.reshape(4, 32, 128)
    pl.semaphore_wait(barrier, count)

    def sem(i):
        return sems.at[i]

    def n1(p, j):
        return p * 3 + j

    def nt(j):
        return 6 + j

    def n2(p, j, t):
        return 9 + (p * 3 + j) * 2 + t

    def n3(p, j, t):
        return 21 + (p * 3 + j) * 2 + t

    RB = 33

    def settle(dummy, ssem, rsem):
        done = remote(dummy, dummy, ssem, rsem, device(pos, other))
        done.wait_recv()
        done.wait_send()

    def here(src, dst, s):
        return pltpu.make_async_copy(src, dst, s)

    def stage1(p):
        for j in range(3):
            ra = ROLES[j][0]
            me = pos[ra]
            src = data[p].at[:, pl.ds(OFF[j], WID[j])]
            for d in (1, 2, 3):
                dev = device(moved(pos, ra, d), core)
                if p == 0:
                    to = lax.rem(me + d, 4)
                    remote(tab.at[j, to], tabr.at[j, me], sem(nt(j)), sem(RB + nt(j)), dev).start()
                remote(src, ag[j].at[p, me], sem(n1(p, j)), sem(RB + n1(p, j)), dev).start()
            if p == 0:
                here(tab.at[j, me], tabr.at[j, me], sem(2 * RB + nt(j))).start()
            here(src, ag[j].at[p, me], sem(2 * RB + n1(p, j))).start()

    def wait1(p, j):
        if p == 0:
            settle(tabr.at[j, pl.ds(0, 3)], sem(nt(j)), sem(RB + nt(j)))
            here(tab.at[j, 0], tabr.at[j, 0], sem(2 * RB + nt(j))).wait()
        settle(ag[j].at[p, pl.ds(0, 3)], sem(n1(p, j)), sem(RB + n1(p, j)))
        here(ag[j].at[p, 0], ag[j].at[p, 0], sem(2 * RB + n1(p, j))).wait()

    sub3 = lax.broadcasted_iota(jnp.int32, (32, 8, 128), 1).astype(F32)

    def build_masks(j):
        wt_acc = jnp.zeros((32, 8, 1), F32)
        for a in range(4):
            code = jnp.broadcast_to(tabr[j, a, 0].reshape(32, 1, 128), (32, 8, 128))
            wgt = jnp.broadcast_to(tabr[j, a, 1].reshape(32, 1, 128), (32, 8, 128))
            hit = jnp.where(code == sub3, 1.0, 0.0)
            pm[j, a] = hit.reshape(256, 128).astype(BF16)
            wmain[j, a] = jnp.sum(hit * wgt, axis=2, keepdims=True).reshape(256, 1)
            for h in range(2):
                mine = jnp.where((code == 8.0) & (sub3 == float(h * 4 + a)), 1.0, 0.0)
                pm[j, 4 + h * 4 + a] = mine.reshape(256, 128).astype(BF16)
                wt_acc = wt_acc + jnp.sum(mine * wgt, axis=2, keepdims=True)
        wtail[j] = wt_acc.reshape(256, 1)

    def pack(p, j):
        half = WID[j] // 2

        def per_block(a, carry):
            for s, n in cols(j):
                res = jnp.dot(pm[j, a], ag[j][p, a, :, s : s + n], preferred_element_type=F32)
                if p == 0:
                    res = res * wmain[j, a]
                send2[j][:, :, a, :, s : s + n] = res.reshape(4, 8, 8, n).astype(BF16)
            return carry

        lax.fori_loop(0, 4, per_block, 0)

        def per_cols(i, carry):
            s = pl.multiple_of(i * 128, 128)
            res = jnp.zeros((256, 128), F32)
            for h in range(2):
                for a in range(4):
                    src = ag[j][p, a, :, pl.ds(pl.multiple_of(h * half + s, 128), 128)]
                    res = res + jnp.dot(pm[j, 4 + h * 4 + a], src, preferred_element_type=F32)
            if p == 0:
                res = res * wtail[j]
            send2t[j][:, :, :, pl.ds(s, 128)] = res.reshape(4, 8, 8, 128).astype(BF16)
            return carry

        lax.fori_loop(0, half // 128, per_cols, 0)

    def stage2(p, j):
        rb = ROLES[j][1]
        me = pos[rb]
        for t, (a, b) in enumerate(((send2, recv2), (send2t, recv2t))):
            for d in (1, 2, 3):
                to = lax.rem(me + d, 4)
                dev = device(moved(pos, rb, d), core)
                remote(a[j].at[to], b[j].at[p, me], sem(n2(p, j, t)), sem(RB + n2(p, j, t)), dev).start()
            here(a[j].at[me], b[j].at[p, me], sem(2 * RB + n2(p, j, t))).start()

    def wait2(p, j):
        for t, ref in ((0, recv2), (1, recv2t)):
            settle(ref[j].at[p, pl.ds(0, 3)], sem(n2(p, j, t)), sem(RB + n2(p, j, t)))
            here(ref[j].at[p, 0], ref[j].at[p, 0], sem(2 * RB + n2(p, j, t))).wait()

    def stage3(p, j):
        ra, rb, rc = ROLES[j]
        for d in (1, 2, 3, 0):
            dst_pos = moved(pos, rc, d)
            for flip in (0, 1):
                k = core if flip == 0 else other
                ck = dst_pos[rc] * 2 + k
                dev = device(dst_pos, k)
                for b in range(4):
                    src = recv2[j].at[p, b, ck]
                    dst = main_at(mains[p], j, b, pos[rc], core)
                    if d == 0 and flip == 0:
                        here(src, dst, sem(2 * RB + n3(p, j, 0))).start()
                    else:
                        remote(src, dst, sem(n3(p, j, 0)), sem(RB + n3(p, j, 0)), dev).start()
                src = recv2t[j].at[p, :, ck]
                dst = tails[p][j].at[pos[rc] * 2 + core]
                if d == 0 and flip == 0:
                    here(src, dst, sem(2 * RB + n3(p, j, 1))).start()
                else:
                    remote(src, dst, sem(n3(p, j, 1)), sem(RB + n3(p, j, 1)), dev).start()

    def wait3(p, j):
        for t, ref in ((0, recv2), (1, recv2t)):
            settle(ref[j].at[p, :, pl.ds(0, 7)], sem(n3(p, j, t)), sem(RB + n3(p, j, t)))
            dummy = ref[j].at[p, :, 0]
            here(dummy, dummy, sem(2 * RB + n3(p, j, t))).wait()

    RR = 15

    def rsem(i):
        return rsems.at[i]

    def m1(j, t):
        return j * 2 + t

    def m2(j, t):
        return 6 + j * 2 + t

    def back1(j):
        ra, rb, rc = ROLES[j]
        mine = pos[rc] * 2 + core
        for d in (1, 2, 3, 0):
            dst_pos = moved(pos, rc, d)
            for flip in (0, 1):
                k = core if flip == 0 else other
                ck = dst_pos[rc] * 2 + k
                dev = device(dst_pos, k)
                local_copy = d == 0 and flip == 0
                for b in range(4):
                    src = main_at(rmain, j, b, dst_pos[rc], k)
                    dst = r1[j].at[b, mine]
                    if local_copy:
                        here(src, dst, rsem(2 * RR + m1(j, 0))).start()
                    else:
                        remote(src, dst, rsem(m1(j, 0)), rsem(RR + m1(j, 0)), dev).start()
                src = rtails[j].at[ck]
                dst = r1t[j].at[:, mine]
                if local_copy:
                    here(src, dst, rsem(2 * RR + m1(j, 1))).start()
                else:
                    remote(src, dst, rsem(m1(j, 1)), rsem(RR + m1(j, 1)), dev).start()

    def back_wait1(j):
        for t, ref in ((0, r1), (1, r1t)):
            settle(ref[j].at[:, pl.ds(0, 7)], rsem(m1(j, t)), rsem(RR + m1(j, t)))
            dummy = ref[j].at[:, 0]
            here(dummy, dummy, rsem(2 * RR + m1(j, t))).wait()

    def back2(j):
        rb = ROLES[j][1]
        me = pos[rb]
        for t, (a, b) in enumerate(((r1, r2), (r1t, r2t_hbm))):
            for d in (1, 2, 3):
                to = lax.rem(me + d, 4)
                dev = device(moved(pos, rb, d), core)
                remote(a[j].at[to], b[j].at[me], rsem(m2(j, t)), rsem(RR + m2(j, t)), dev).start()
            here(a[j].at[me], b[j].at[me], rsem(2 * RR + m2(j, t))).start()

    def back_wait2(j):
        for t, ref in ((0, r2), (1, r2t_hbm)):
            settle(ref[j].at[pl.ds(0, 3)], rsem(m2(j, t)), rsem(RR + m2(j, t)))
            here(ref[j].at[0], ref[j].at[0], rsem(2 * RR + m2(j, t))).wait()

    def fold(j):
        ra = ROLES[j][0]
        half = WID[j] // 2
        cp = here(r2t_hbm[j], send2t[j], lsems.at[0])
        cp.start()
        cp.wait()

        def per_cols(i, carry):
            s = pl.multiple_of(i * 128, 128)
            tail = flat(send2t[j][:, :, :, pl.ds(s, 128)])
            for d in range(4):
                a = lax.rem(pos[ra] + d, 4)
                for h in range(2):
                    s0 = pl.multiple_of(h * half + s, 128)
                    rows = flat(r2[j][:, :, a, :, pl.ds(s0, 128)])
                    res = mm(pm[j, a], rows, 0, 0) + mm(pm[j, 4 + h * 4 + a], tail, 0, 0)
                    if d == 0:
                        own[:, pl.ds(pl.multiple_of(OFF[j] + s0, 128), 128)] = res
                    else:
                        ag[j][1, d - 1, :, pl.ds(s0, 128)] = res.astype(BF16)
            return carry

        lax.fori_loop(0, half // 128, per_cols, 0)

    def back3(j):
        ra = ROLES[j][0]
        for d in (1, 2, 3):
            dev = device(moved(pos, ra, d), core)
            remote(ag[j].at[1, d - 1], got[j].at[d - 1], rsem(12 + j), rsem(RR + 12 + j), dev).start()

    def finish(j):
        settle(got[j], rsem(12 + j), rsem(RR + 12 + j))
        for s, n in cols(j):
            total = own[:, OFF[j] + s : OFF[j] + s + n]
            for d in range(3):
                total = total + got[j][d, :, s : s + n].astype(F32)
            out[:, OFF[j] + s : OFF[j] + s + n] = total.astype(BF16)

    def tail_picks(j, swap):
        shape = (256, 128) if swap else (128, 256)
        i = lax.broadcasted_iota(jnp.int32, shape, 0 if swap else 1)
        n = lax.broadcasted_iota(jnp.int32, shape, 1 if swap else 0)
        block, half = rows_of(i)[j]
        return [jnp.where((block == n) & (half == h), 1.0, 0.0).astype(BF16) for h in range(2)]

    def load_tail(p, dst, stage):
        for j in range(3):
            w = WID[j] // 2
            cp = here(tails[p][j], stage.at[:, :, :, pl.ds(0, w)], lsems.at[0])
            cp.start()
            cp.wait()
            picks = tail_picks(j, False)
            for s in range(0, w, 128):
                rows = flat(stage[:, :, :, s : s + 128])
                for h in range(2):
                    o = OFF[j] + h * w + s
                    dst[0:128, o : o + 128] = mm(picks[h], rows, 1, 0).astype(BF16)

    wide[0:16] = ga[...]
    wide[16:32] = ua[...]
    narrow[0, 0:16] = go[...]
    narrow[0, 16:32] = jnp.zeros_like(go)
    narrow[1, 0:16] = jnp.zeros_like(uo)
    narrow[1, 16:32] = uo[...]
    for ref in (acc_do, acc_di, acc_in, acc_o):
        ref[...] = jnp.zeros_like(ref)

    stage1(0)
    stage1(1)
    for j in range(3):
        wait1(0, j)
        build_masks(j)
        pack(0, j)
        stage2(0, j)
    for j in range(3):
        wait2(0, j)
        stage3(0, j)

    def first_half(gate_pre, up_pre, wd, slab, gc, stage):
        loads = [
            here(gate_hbm, gate_pre, lsems.at[1]),
            here(up_hbm, up_pre, lsems.at[2]),
            here(wd_hbm, wd, lsems.at[3]),
        ]
        for cp in loads:
            cp.start()
        for j in range(3):
            wait1(1, j)
            pack(1, j)
            stage2(1, j)
        for cp in loads:
            cp.wait()
        for j in range(3):
            wait3(0, j)

        def rows_at(r0, n, order):
            gate = jnp.dot(order, gate_pre[...], preferred_element_type=F32)
            up = jnp.dot(order, up_pre[...], preferred_element_type=F32)
            sig = jax.nn.sigmoid(gate)
            silu = gate * sig
            hidden = (silu * up).astype(BF16)
            g = gc[0:n]
            dlora[pl.ds(r0, n)] = mm(hidden, da[...], 1, 1).astype(BF16)
            gl = mm(g, do[...], 1, 1).astype(BF16)
            acc_di[...] += mm(gl, hidden, 0, 0)
            gh = mm(g, wd[...], 1, 1) + adapter_scale * mm(gl, da[...], 1, 0)
            gate_grad = (gh * up * sig * (1.0 + gate * (1.0 - sig))).astype(BF16)
            up_grad = (gh * silu).astype(BF16)
            gg[pl.ds(r0, n)] = gate_grad
            gu[pl.ds(r0, n)] = up_grad
            both = mm(gate_grad, narrow[0], 1, 1) + mm(up_grad, narrow[1], 1, 1)
            back[pl.ds(r0, n)] = both.astype(BF16)

        def main_rows(c, carry):
            cp = here(gmain.at[c], slab, lsems.at[0])
            cp.start()
            i = lax.broadcasted_iota(jnp.int32, (256, 1152), 0)
            n = lax.broadcasted_iota(jnp.int32, (256, 1152), 1)
            order = jnp.where(slot_of(c * 32 + i // 8, i % 8) == n, 1.0, 0.0).astype(BF16)
            cp.wait()
            for s in range(0, 4096, 512):
                gc[:, s : s + 512] = flat(slab[:, :, :, :, s : s + 512])
            rows_at(pl.multiple_of(c * 256, 256), 256, order)
            return carry

        lax.fori_loop(0, 4, main_rows, 0)
        for j in range(3):
            wait2(1, j)
            stage3(1, j)
        load_tail(0, gtail, stage)
        i = lax.broadcasted_iota(jnp.int32, (128, 1152), 0)
        n = lax.broadcasted_iota(jnp.int32, (128, 1152), 1)
        gc[0:128] = gtail[...]
        rows_at(1024, 128, jnp.where(slot_of(i, 8) == n, 1.0, 0.0).astype(BF16))

    pl.run_scoped(
        first_half,
        pltpu.VMEM((1152, 768), BF16),
        pltpu.VMEM((1152, 768), BF16),
        pltpu.VMEM((768, 4096), BF16),
        pltpu.VMEM((4, 4, 2, 8, 4096), BF16),
        pltpu.VMEM((256, 4096), BF16),
        pltpu.VMEM((8, 4, 8, 768), BF16),
    )

    def second_half(wgu, ro, tail_out, tail_pack):
        for j in range(3):
            w = WID[j]
            half = w // 2
            loads = [
                here(src.at[pl.ds(OFF[j], w)], wgu.at[t, pl.ds(0, w)], lsems.at[1 + t])
                for t, src in enumerate((wg_hbm, wu_hbm))
            ]
            for cp in loads:
                cp.start()
            for cp in loads:
                cp.wait()

            def per_cols(i, carry):
                s = pl.multiple_of(i * CHUNK, CHUNK)
                o = pl.multiple_of(OFF[j] + s, CHUNK)
                slot = lax.rem(i, 2)

                def rows(r0, n):
                    res = mm(gg[r0 : r0 + n], wgu[0, pl.ds(s, CHUNK)], 1, 1)
                    res = res + mm(gu[r0 : r0 + n], wgu[1, pl.ds(s, CHUNK)], 1, 1)
                    return res + adapter_scale * mm(back[r0 : r0 + n], wide[:, pl.ds(o, CHUNK)], 1, 0)

                @pl.when(i >= 2)
                def _():
                    here(ro.at[0], rmain.at[:, :, :, :, :, pl.ds(0, CHUNK)], lsems.at[3 + slot]).wait()

                for x in range(4):
                    ro[slot, x] = rows(x * 256, 256).reshape(4, 4, 2, 8, CHUNK).astype(BF16)
                tail_out[:, pl.ds(s, CHUNK)] = rows(1024, 128).astype(BF16)
                here(ro.at[slot], rmain.at[:, :, :, :, :, pl.ds(o, CHUNK)], lsems.at[3 + slot]).start()
                return carry

            lax.fori_loop(0, w // CHUNK, per_cols, 0)
            picks = tail_picks(j, True)
            for s in range(0, half, 128):
                res = mm(picks[0], tail_out[:, s : s + 128], 1, 0)
                res = res + mm(picks[1], tail_out[:, half + s : half + s + 128], 1, 0)
                tail_pack[:, :, :, s : s + 128] = res.reshape(8, 4, 8, 128).astype(BF16)
            cp = here(tail_pack.at[:, :, :, pl.ds(0, half)], rtails[j], lsems.at[0])
            cp.start()
            for slot in range(2):
                here(ro.at[0], rmain.at[:, :, :, :, :, pl.ds(0, CHUNK)], lsems.at[3 + slot]).wait()
            cp.wait()
            back1(j)

    pl.run_scoped(
        second_half,
        pltpu.VMEM((2, 1536, 768), BF16),
        pltpu.VMEM((2, 4, 4, 4, 2, 8, CHUNK), BF16),
        pltpu.VMEM((128, 1536), BF16),
        pltpu.VMEM((8, 4, 8, 768), BF16),
    )

    for j in range(3):
        wait3(1, j)

    def adapters(slab, xc, gc, stage):
        def add(r0, n, g, x):
            deltas = mm(x, wide[...], 1, 1).astype(BF16)
            acc_o[0] += mm(deltas, gg[pl.ds(r0, n)], 0, 0)
            acc_o[1] += mm(deltas, gu[pl.ds(r0, n)], 0, 0)
            lora = back[pl.ds(r0, n)]
            down = dlora[pl.ds(r0, n)]
            acc_in[...] += mm(lora, x, 0, 0)
            acc_do[...] += mm(down, g, 0, 0)

        def main_rows(c, carry):
            cps = [here(gmain.at[c], slab.at[0], lsems.at[1]), here(xmain.at[c], slab.at[1], lsems.at[2])]
            for cp in cps:
                cp.start()
            for cp in cps:
                cp.wait()
            for s in range(0, 4096, 512):
                gc[:, s : s + 512] = flat(slab[0, :, :, :, :, s : s + 512])
                xc[:, s : s + 512] = flat(slab[1, :, :, :, :, s : s + 512])
            add(pl.multiple_of(c * 256, 256), 256, gc[...], xc[...])
            return carry

        lax.fori_loop(0, 4, main_rows, 0)
        for j in range(3):
            back_wait1(j)
            back2(j)
        load_tail(1, xc, stage)
        add(1024, 128, gtail[...], xc[0:128])

    pl.run_scoped(
        adapters,
        pltpu.VMEM((2, 4, 4, 2, 8, 4096), BF16),
        pltpu.VMEM((256, 4096), BF16),
        pltpu.VMEM((256, 4096), BF16),
        pltpu.VMEM((8, 4, 8, 768), BF16),
    )
    o_gi[...] = (adapter_scale * acc_in[0:16]).astype(BF16)
    o_ui[...] = (adapter_scale * acc_in[16:32]).astype(BF16)
    o_go[...] = (adapter_scale * acc_o[0, 0:16]).astype(BF16)
    o_uo[...] = (adapter_scale * acc_o[1, 16:32]).astype(BF16)
    o_di[...] = (adapter_scale * acc_di[...]).astype(BF16)
    o_do[...] = (adapter_scale * acc_do[...]).astype(BF16)

    for j in range(3):
        back_wait2(j)
        fold(j)
        back3(j)
    for j in range(3):
        finish(j)


def whole_block(*operands):
    any_spec = pl.BlockSpec(memory_space=pl.ANY)
    vmem = pl.BlockSpec(memory_space=pltpu.VMEM)

    def shape(*dims):
        return jax.ShapeDtypeStruct(dims, BF16)

    outs = [shape(128, 4096), shape(16, 4096), shape(16, 768), shape(16, 4096), shape(16, 768)]
    outs += [shape(16, 768), shape(16, 4096)]
    tmp = [shape(4, 4, 4, 2, 8, 4096)] * 3
    tmp += [shape(8, 4, 8, w // 2) for w in WID] * 3
    tmp += [shape(2, 4, 8, 4, 8, w) for w in WID]
    tmp += [shape(2, 4, 8, 8, w // 2) for w in WID]
    tmp += [shape(4, 8, 4, 8, w) for w in WID]
    tmp += [shape(4, 8, 8, w // 2) for w in WID] * 2
    scratch = [pltpu.VMEM((2, 4, 128, w), BF16) for w in WID]
    scratch += [pltpu.VMEM((4, 8, 4, 8, w), BF16) for w in WID]
    scratch += [pltpu.VMEM((4, 8, 8, w // 2), BF16) for w in WID]
    scratch += [pltpu.VMEM((4, 8, 4, 8, w), BF16) for w in WID]
    scratch += [pltpu.VMEM((3, 128, w), BF16) for w in WID]
    scratch += [
        pltpu.VMEM((3, 4, 2, 32, 128), F32),
        pltpu.VMEM((3, 4, 2, 32, 128), F32),
        pltpu.VMEM((3, 12, 256, 128), BF16),
        pltpu.VMEM((3, 4, 256, 1), F32),
        pltpu.VMEM((3, 256, 1), F32),
        pltpu.VMEM((128, 4096), F32),
        pltpu.VMEM((1152, 768), BF16),
        pltpu.VMEM((1152, 768), BF16),
        pltpu.VMEM((128, 4096), BF16),
        pltpu.VMEM((1152, 16), BF16),
        pltpu.VMEM((1152, 32), BF16),
        pltpu.VMEM((16, 4096), F32),
        pltpu.VMEM((16, 768), F32),
        pltpu.VMEM((32, 4096), F32),
        pltpu.VMEM((2, 32, 768), F32),
        pltpu.VMEM((32, 4096), BF16),
        pltpu.VMEM((2, 32, 768), BF16),
        pltpu.SemaphoreType.DMA((99,)),
        pltpu.SemaphoreType.DMA((45,)),
        pltpu.SemaphoreType.DMA((5,)),
    ]
    res = pl.pallas_call(
        block_kernel,
        out_shape=outs + tmp,
        in_specs=[vmem] * 2 + [any_spec] * 7 + [vmem] * 6,
        out_specs=[vmem] * N_OUT + [any_spec] * N_TMP,
        scratch_shapes=scratch,
        compiler_params=pltpu.CompilerParams(
            collective_id=0, has_side_effects=True, vmem_limit_bytes=67043328
        ),
        name="whole_block",
    )(*operands)
    return res[:N_OUT]


def local(rows, grad, choice, weight, wg, wu, wd, ga, go, ua, uo, da, do, gate_pre, up_pre):
    res = whole_block(
        choice.T, weight.T, grad, rows, gate_pre[0], up_pre[0], wg[0], wu[0], wd[0],
        ga[0], go[0], ua[0], uo[0], da[0], do[0],
    )
    return (res[0],) + tuple(v[None] for v in res[1:])


def solution(mesh):
    row = P(("ctx", "ep"), None)
    cube = P(("ctx", "ep"), None, None)
    return jax.shard_map(
        local,
        mesh=mesh,
        in_specs=(row,) * 4 + (cube,) * 11,
        out_specs=(row,) + (cube,) * 6,
        check_vma=False,
    )
```

time: 421 us -> 311 us (0.74); the launches traced: 415 us -> 310 us
  matrix products: 105 us -> 0 us
  local copies, waits for them, and re-layouts: 5.44 us -> 11 us
    dot_general x44 -> x0, matrix products: 105 us -> none  [the longest x24 72.1 us: mm(): lax.dot_general(a, b, (((da,), (db,)), ((), ())), preferred_element_type=...]
    unnamed x57 -> x7, local copies, waits for them, and re-layouts: 2.46 us -> 11 us
    pallas_call x2 -> x1, Pallas kernels: 302 us -> 298 us  [whole_block(): pl.pallas_call(block_kernel, out_shape=outs + tmp, in_specs=[vmem] * 2 +...]
where the time goes in v2:
time: 311 us; the launch traced here: 310 us
  Pallas kernels  298 us (96%)
  local copies, waits for them, and re-layouts  11 us (4%)
    pallas_call x1, Pallas kernels, whole_block(): pl.pallas_call(block_kernel, out_shape=outs + tmp, in_specs=[vmem] * 2 +...  298 us
    unnamed x7, local copies, waits for them, and re-layouts  11 us

profile of v2, /device:TPU:1, one launch (start us, length us, event | category | flops | bytes accessed | tf_op | source)
XLA Modules:
  0.0 309.9 jit_solution(934511709473016577)
XLA Ops:
  0.6 298.2 %whole_block.1 = (bf16[128,4096]{1,0:T(8,128)(2,1)}, bf16[16,4096]{1,0:T(8,128)(2,1)}, bf16[16,768]{1,0:T(8,128)(2,1)}, bf16[16,4096]{1,0:T(8,128)(2,1)}, bf16[1...) custom-call(s32[8,128]{1,0:T(8,128)} %bitcast.36, ...), custom_call_target="tpu_custom_call" | custom-call | tf_op jit(solution)/shard_map/whole_block/pallas_call | solution.py:633
  298.9 2.3 copy.29
  301.2 1.6 copy.30
  302.7 1.3 copy.31
  304.1 1.6 copy.32
  305.7 1.3 copy.33
  307.0 1.3 copy.34
  308.3 1.6 copy.35

commit v3 on v2

--- a/solution.py
+++ b/solution.py
@@ -7,8 +7,9 @@
 
 MESH = pl.DeviceIdType.MESH
 ROLES = ((0, 1, 2), (1, 2, 0), (2, 0, 1))
-WID = (1280, 1280, 1536)
-OFF = (0, 1280, 2560)
+WID = (1408, 1408, 1280)
+OFF = (0, 1408, 2816)
+HALF = ((768, 640), (768, 640), (640, 640))
 CHUNK = 256
 F32 = jnp.float32
 BF16 = jnp.bfloat16
@@ -76,7 +77,12 @@
 
 
 def cols(j):
-    return [(s, CHUNK) for s in range(0, WID[j], CHUNK)]
+    return [(s, min(CHUNK, WID[j] - s)) for s in range(0, WID[j], CHUNK)]
+
+
+def halves(j, s):
+    h0, h1 = HALF[j]
+    return (s, h0 + s) if s < h1 else (s,)
 
 
 def rows_of(i):
@@ -122,7 +128,7 @@
     r2t_hbm = tmp[24:27]
     sc = refs[N_IN + N_OUT + N_TMP :]
     ag, send2, send2t, r2, got = sc[0:3], sc[3:6], sc[6:9], sc[9:12], sc[12:15]
-    (tab, tabr, pm, wmain, wtail, own, gg, gu, gtail, dlora, back, acc_do, acc_di, acc_in, acc_o, wide, narrow, sems, rsems, lsems) = sc[15:]
+    (tab, tabr, pm, wmain, wtail, own, gg, gu, gtail, dlora, back, acc_do, acc_di, acc_in, acc_o, wide, narrow, tflat, sems, rsems, lsems) = sc[15:]
     mains = (gmain, xmain)
     data = (g_hbm, x_hbm)
     pos, core = coords()
@@ -210,7 +216,7 @@
         wtail[j] = wt_acc.reshape(256, 1)
 
     def pack(p, j):
-        half = WID[j] // 2
+        h0, h1 = HALF[j]
 
         def per_block(a, carry):
             for s, n in cols(j):
@@ -222,19 +228,23 @@
 
         lax.fori_loop(0, 4, per_block, 0)
 
-        def per_cols(i, carry):
-            s = pl.multiple_of(i * 128, 128)
+        def tail_cols(s, n):
             res = jnp.zeros((256, 128), F32)
-            for h in range(2):
+            for h in range(n):
                 for a in range(4):
-                    src = ag[j][p, a, :, pl.ds(pl.multiple_of(h * half + s, 128), 128)]
+                    src = ag[j][p, a, :, pl.ds(pl.multiple_of(h * h0 + s, 128), 128)]
                     res = res + jnp.dot(pm[j, 4 + h * 4 + a], src, preferred_element_type=F32)
             if p == 0:
                 res = res * wtail[j]
             send2t[j][:, :, :, pl.ds(s, 128)] = res.reshape(4, 8, 8, 128).astype(BF16)
+
+        def per_cols(i, carry):
+            tail_cols(pl.multiple_of(i * 128, 128), 2)
             return carry
 
-        lax.fori_loop(0, half // 128, per_cols, 0)
+        lax.fori_loop(0, h1 // 128, per_cols, 0)
+        for s in range(h1, h0, 128):
+            tail_cols(s, 1)
 
     def stage2(p, j):
         rb = ROLES[j][1]
@@ -337,27 +347,35 @@
 
     def fold(j):
         ra = ROLES[j][0]
-        half = WID[j] // 2
+        h0, h1 = HALF[j]
         cp = here(r2t_hbm[j], send2t[j], lsems.at[0])
         cp.start()
         cp.wait()
-
-        def per_cols(i, carry):
-            s = pl.multiple_of(i * 128, 128)
-            tail = flat(send2t[j][:, :, :, pl.ds(s, 128)])
-            for d in range(4):
-                a = lax.rem(pos[ra] + d, 4)
-                for h in range(2):
-                    s0 = pl.multiple_of(h * half + s, 128)
+        for s in range(0, h0, 128):
+            tflat[:, s : s + 128] = flat(send2t[j][:, :, :, s : s + 128])
+        for d in range(4):
+            a = lax.rem(pos[ra] + d, 4)
+            mt = pm[j, a].T
+            tails_mt = [pm[j, 4 + h * 4 + a].T for h in range(2)]
+
+            def fold_cols(s, n):
+                tail = tflat[:, pl.ds(s, 128)]
+                for h in range(n):
+                    s0 = pl.multiple_of(h * h0 + s, 128)
                     rows = flat(r2[j][:, :, a, :, pl.ds(s0, 128)])
-                    res = mm(pm[j, a], rows, 0, 0) + mm(pm[j, 4 + h * 4 + a], tail, 0, 0)
+                    res = mm(mt, rows, 1, 0) + mm(tails_mt[h], tail, 1, 0)
                     if d == 0:
                         own[:, pl.ds(pl.multiple_of(OFF[j] + s0, 128), 128)] = res
                     else:
                         ag[j][1, d - 1, :, pl.ds(s0, 128)] = res.astype(BF16)
-            return carry
-
-        lax.fori_loop(0, half // 128, per_cols, 0)
+
+            def per_cols(i, carry):
+                fold_cols(pl.multiple_of(i * 128, 128), 2)
+                return carry
+
+            lax.fori_loop(0, h1 // 128, per_cols, 0)
+            for s in range(h1, h0, 128):
+                fold_cols(s, 1)
 
     def back3(j):
         ra = ROLES[j][0]
@@ -382,15 +400,15 @@
 
     def load_tail(p, dst, stage):
         for j in range(3):
-            w = WID[j] // 2
+            w = HALF[j][0]
             cp = here(tails[p][j], stage.at[:, :, :, pl.ds(0, w)], lsems.at[0])
             cp.start()
             cp.wait()
             picks = tail_picks(j, False)
             for s in range(0, w, 128):
                 rows = flat(stage[:, :, :, s : s + 128])
-                for h in range(2):
-                    o = OFF[j] + h * w + s
+                for h, o in enumerate(halves(j, s)):
+                    o = OFF[j] + o
                     dst[0:128, o : o + 128] = mm(picks[h], rows, 1, 0).astype(BF16)
 
     wide[0:16] = ga[...]
@@ -480,10 +498,10 @@
         pltpu.VMEM((8, 4, 8, 768), BF16),
     )
 
-    def second_half(wgu, ro, tail_out, tail_pack):
+    def second_half(wgu, ro, ro_last, tail_out, tail_pack):
         for j in range(3):
             w = WID[j]
-            half = w // 2
+            h0, h1 = HALF[j]
             loads = [
                 here(src.at[pl.ds(OFF[j], w)], wgu.at[t, pl.ds(0, w)], lsems.at[1 + t])
                 for t, src in enumerate((wg_hbm, wu_hbm))
@@ -493,44 +511,56 @@
             for cp in loads:
                 cp.wait()
 
+            def rows(r0, n, s, width):
+                o = pl.multiple_of(OFF[j] + s, 128)
+                res = mm(gg[r0 : r0 + n], wgu[0, pl.ds(s, width)], 1, 1)
+                res = res + mm(gu[r0 : r0 + n], wgu[1, pl.ds(s, width)], 1, 1)
+                return res + adapter_scale * mm(back[r0 : r0 + n], wide[:, pl.ds(o, width)], 1, 0)
+
             def per_cols(i, carry):
                 s = pl.multiple_of(i * CHUNK, CHUNK)
-                o = pl.multiple_of(OFF[j] + s, CHUNK)
+                o = pl.multiple_of(OFF[j] + s, 128)
                 slot = lax.rem(i, 2)
-
-                def rows(r0, n):
-                    res = mm(gg[r0 : r0 + n], wgu[0, pl.ds(s, CHUNK)], 1, 1)
-                    res = res + mm(gu[r0 : r0 + n], wgu[1, pl.ds(s, CHUNK)], 1, 1)
-                    return res + adapter_scale * mm(back[r0 : r0 + n], wide[:, pl.ds(o, CHUNK)], 1, 0)
 
                 @pl.when(i >= 2)
                 def _():
                     here(ro.at[0], rmain.at[:, :, :, :, :, pl.ds(0, CHUNK)], lsems.at[3 + slot]).wait()
 
                 for x in range(4):
-                    ro[slot, x] = rows(x * 256, 256).reshape(4, 4, 2, 8, CHUNK).astype(BF16)
-                tail_out[:, pl.ds(s, CHUNK)] = rows(1024, 128).astype(BF16)
+                    ro[slot, x] = rows(x * 256, 256, s, CHUNK).reshape(4, 4, 2, 8, CHUNK).astype(BF16)
+                tail_out[:, pl.ds(s, CHUNK)] = rows(1024, 128, s, CHUNK).astype(BF16)
                 here(ro.at[slot], rmain.at[:, :, :, :, :, pl.ds(o, CHUNK)], lsems.at[3 + slot]).start()
                 return carry
 
             lax.fori_loop(0, w // CHUNK, per_cols, 0)
+            s = w // CHUNK * CHUNK
+            if s < w:
+                last = here(ro_last, rmain.at[:, :, :, :, :, pl.ds(OFF[j] + s, 128)], lsems.at[5])
+                for x in range(4):
+                    ro_last[x] = rows(x * 256, 256, s, 128).reshape(4, 4, 2, 8, 128).astype(BF16)
+                tail_out[:, s:w] = rows(1024, 128, s, 128).astype(BF16)
+                last.start()
             picks = tail_picks(j, True)
-            for s in range(0, half, 128):
+            for s in range(0, h0, 128):
                 res = mm(picks[0], tail_out[:, s : s + 128], 1, 0)
-                res = res + mm(picks[1], tail_out[:, half + s : half + s + 128], 1, 0)
+                if s < h1:
+                    res = res + mm(picks[1], tail_out[:, h0 + s : h0 + s + 128], 1, 0)
                 tail_pack[:, :, :, s : s + 128] = res.reshape(8, 4, 8, 128).astype(BF16)
-            cp = here(tail_pack.at[:, :, :, pl.ds(0, half)], rtails[j], lsems.at[0])
+            cp = here(tail_pack.at[:, :, :, pl.ds(0, h0)], rtails[j], lsems.at[0])
             cp.start()
             for slot in range(2):
                 here(ro.at[0], rmain.at[:, :, :, :, :, pl.ds(0, CHUNK)], lsems.at[3 + slot]).wait()
             cp.wait()
+            if w % CHUNK:
+                last.wait()
             back1(j)
 
     pl.run_scoped(
         second_half,
-        pltpu.VMEM((2, 1536, 768), BF16),
+        pltpu.VMEM((2, 1408, 768), BF16),
         pltpu.VMEM((2, 4, 4, 4, 2, 8, CHUNK), BF16),
-        pltpu.VMEM((128, 1536), BF16),
+        pltpu.VMEM((4, 4, 4, 2, 8, 128), BF16),
+        pltpu.VMEM((128, 1408), BF16),
         pltpu.VMEM((8, 4, 8, 768), BF16),
     )
 
@@ -598,14 +628,14 @@
     outs = [shape(128, 4096), shape(16, 4096), shape(16, 768), shape(16, 4096), shape(16, 768)]
     outs += [shape(16, 768), shape(16, 4096)]
     tmp = [shape(4, 4, 4, 2, 8, 4096)] * 3
-    tmp += [shape(8, 4, 8, w // 2) for w in WID] * 3
+    tmp += [shape(8, 4, 8, h) for h, _ in HALF] * 3
     tmp += [shape(2, 4, 8, 4, 8, w) for w in WID]
-    tmp += [shape(2, 4, 8, 8, w // 2) for w in WID]
+    tmp += [shape(2, 4, 8, 8, h) for h, _ in HALF]
     tmp += [shape(4, 8, 4, 8, w) for w in WID]
-    tmp += [shape(4, 8, 8, w // 2) for w in WID] * 2
+    tmp += [shape(4, 8, 8, h) for h, _ in HALF] * 2
     scratch = [pltpu.VMEM((2, 4, 128, w), BF16) for w in WID]
     scratch += [pltpu.VMEM((4, 8, 4, 8, w), BF16) for w in WID]
-    scratch += [pltpu.VMEM((4, 8, 8, w // 2), BF16) for w in WID]
+    scratch += [pltpu.VMEM((4, 8, 8, h), BF16) for h, _ in HALF]
     scratch += [pltpu.VMEM((4, 8, 4, 8, w), BF16) for w in WID]
     scratch += [pltpu.VMEM((3, 128, w), BF16) for w in WID]
     scratch += [
@@ -626,9 +656,10 @@
         pltpu.VMEM((2, 32, 768), F32),
         pltpu.VMEM((32, 4096), BF16),
         pltpu.VMEM((2, 32, 768), BF16),
+        pltpu.VMEM((256, 768), BF16),
         pltpu.SemaphoreType.DMA((99,)),
         pltpu.SemaphoreType.DMA((45,)),
-        pltpu.SemaphoreType.DMA((5,)),
+        pltpu.SemaphoreType.DMA((6,)),
     ]
     res = pl.pallas_call(
         block_kernel,
@@ -644,11 +675,28 @@
     return res[:N_OUT]
 
 
+def hand_over_kernel(*refs):
+    for src, dst in zip(refs[:N_OUT], refs[N_OUT:]):
+        dst[...] = src[...]
+
+
+def hand_over(arrays):
+    vmem = pl.BlockSpec(memory_space=pltpu.VMEM)
+    return pl.pallas_call(
+        hand_over_kernel,
+        out_shape=[jax.ShapeDtypeStruct(a.shape, a.dtype) for a in arrays],
+        in_specs=[vmem] * N_OUT,
+        out_specs=[vmem] * N_OUT,
+        name="hand_over",
+    )(*arrays)
+
+
 def local(rows, grad, choice, weight, wg, wu, wd, ga, go, ua, uo, da, do, gate_pre, up_pre):
     res = whole_block(
         choice.T, weight.T, grad, rows, gate_pre[0], up_pre[0], wg[0], wu[0], wd[0],
         ga[0], go[0], ua[0], uo[0], da[0], do[0],
     )
+    res = hand_over(res)
     return (res[0],) + tuple(v[None] for v in res[1:])
 
 

time: 311 us -> 302 us (0.971)
  local copies, waits for them, and re-layouts: 11 us -> 0 us
    unnamed x7 -> x0, local copies, waits for them, and re-layouts: 11 us -> none
where the time goes in v3:
time: 302 us; the launch traced here: 300 us
  Pallas kernels  299 us (99%)
    pallas_call x1, Pallas kernels, whole_block(): pl.pallas_call(block_kernel, out_shape=outs + tmp, in_specs=[vmem] * 2 +...  297 us

profile of v3, /device:TPU:1, one launch (start us, length us, event | category | flops | bytes accessed | tf_op | source)
XLA Modules:
  0.0 299.9 jit_solution(9702903350305693240)
XLA Ops:
  0.6 296.8 %whole_block.1 = (bf16[128,4096]{1,0:T(8,128)(2,1)}, bf16[16,4096]{1,0:T(8,128)(2,1)}, bf16[16,768]{1,0:T(8,128)(2,1)}, bf16[16,4096]{1,0:T(8,128)(2,1)}, bf16[1...) custom-call(s32[8,128]{1,0:T(8,128)} %bitcast.30, ...), custom_call_target="tpu_custom_call" | custom-call | tf_op jit(solution)/shard_map/whole_block/pallas_call | solution.py:664
  297.4 2.5 hand_over.1

commit v4 on v3

--- a/solution.py
+++ b/solution.py
@@ -445,12 +445,26 @@
             stage2(1, j)
         for cp in loads:
             cp.wait()
+
+        def sort_rows(r0, n, block, r):
+            lane = lax.broadcasted_iota(jnp.int32, (n, 1152), 1)
+            order = jnp.where(slot_of(block, r) == lane, 1.0, 0.0).astype(BF16)
+            gg[pl.ds(r0, n)] = jnp.dot(order, gate_pre[...], preferred_element_type=F32).astype(BF16)
+            gu[pl.ds(r0, n)] = jnp.dot(order, up_pre[...], preferred_element_type=F32).astype(BF16)
+
+        def sort_main(c, carry):
+            i = lax.broadcasted_iota(jnp.int32, (256, 1), 0)
+            sort_rows(pl.multiple_of(c * 256, 256), 256, c * 32 + i // 8, i % 8)
+            return carry
+
+        lax.fori_loop(0, 4, sort_main, 0)
+        sort_rows(1024, 128, lax.broadcasted_iota(jnp.int32, (128, 1), 0), 8)
         for j in range(3):
             wait3(0, j)
 
-        def rows_at(r0, n, order):
-            gate = jnp.dot(order, gate_pre[...], preferred_element_type=F32)
-            up = jnp.dot(order, up_pre[...], preferred_element_type=F32)
+        def rows_at(r0, n):
+            gate = gg[pl.ds(r0, n)].astype(F32)
+            up = gu[pl.ds(r0, n)].astype(F32)
             sig = jax.nn.sigmoid(gate)
             silu = gate * sig
             hidden = (silu * up).astype(BF16)
@@ -467,26 +481,25 @@
             back[pl.ds(r0, n)] = both.astype(BF16)
 
         def main_rows(c, carry):
-            cp = here(gmain.at[c], slab, lsems.at[0])
-            cp.start()
-            i = lax.broadcasted_iota(jnp.int32, (256, 1152), 0)
-            n = lax.broadcasted_iota(jnp.int32, (256, 1152), 1)
-            order = jnp.where(slot_of(c * 32 + i // 8, i % 8) == n, 1.0, 0.0).astype(BF16)
-            cp.wait()
+            here(gmain.at[c], slab, lsems.at[0]).wait()
             for s in range(0, 4096, 512):
                 gc[:, s : s + 512] = flat(slab[:, :, :, :, s : s + 512])
-            rows_at(pl.multiple_of(c * 256, 256), 256, order)
+
+            @pl.when(c < 3)
+            def _():
+                here(gmain.at[c + 1], slab, lsems.at[0]).start()
+
+            rows_at(pl.multiple_of(c * 256, 256), 256)
             return carry
 
+        here(gmain.at[0], slab, lsems.at[0]).start()
         lax.fori_loop(0, 4, main_rows, 0)
+        load_tail(0, gtail, stage)
+        gc[0:128] = gtail[...]
+        rows_at(1024, 128)
         for j in range(3):
             wait2(1, j)
             stage3(1, j)
-        load_tail(0, gtail, stage)
-        i = lax.broadcasted_iota(jnp.int32, (128, 1152), 0)
-        n = lax.broadcasted_iota(jnp.int32, (128, 1152), 1)
-        gc[0:128] = gtail[...]
-        rows_at(1024, 128, jnp.where(slot_of(i, 8) == n, 1.0, 0.0).astype(BF16))
 
     pl.run_scoped(
         first_half,
@@ -499,16 +512,19 @@
     )
 
     def second_half(wgu, ro, ro_last, tail_out, tail_pack):
+        def weights(j):
+            w = WID[j]
+            return [
+                here(src.at[pl.ds(OFF[j], w)], wgu.at[t, pl.ds(0, w)], lsems.at[1 + t])
+                for t, src in enumerate((wg_hbm, wu_hbm))
+            ]
+
+        for cp in weights(0):
+            cp.start()
         for j in range(3):
             w = WID[j]
             h0, h1 = HALF[j]
-            loads = [
-                here(src.at[pl.ds(OFF[j], w)], wgu.at[t, pl.ds(0, w)], lsems.at[1 + t])
-                for t, src in enumerate((wg_hbm, wu_hbm))
-            ]
-            for cp in loads:
-                cp.start()
-            for cp in loads:
+            for cp in weights(j):
                 cp.wait()
 
             def rows(r0, n, s, width):
@@ -540,6 +556,9 @@
                     ro_last[x] = rows(x * 256, 256, s, 128).reshape(4, 4, 2, 8, 128).astype(BF16)
                 tail_out[:, s:w] = rows(1024, 128, s, 128).astype(BF16)
                 last.start()
+            if j < 2:
+                for cp in weights(j + 1):
+                    cp.start()
             picks = tail_picks(j, True)
             for s in range(0, h0, 128):
                 res = mm(picks[0], tail_out[:, s : s + 128], 1, 0)
@@ -589,10 +608,11 @@
             add(pl.multiple_of(c * 256, 256), 256, gc[...], xc[...])
             return carry
 
-        lax.fori_loop(0, 4, main_rows, 0)
+        lax.fori_loop(0, 2, main_rows, 0)
         for j in range(3):
             back_wait1(j)
             back2(j)
+        lax.fori_loop(2, 4, main_rows, 0)
         load_tail(1, xc, stage)
         add(1024, 128, gtail[...], xc[0:128])
 

time: 302 us -> 300 us (level)
  no operation moved by 1% of the time
where the time goes in v4:
time: 300 us
  Pallas kernels  299 us (100%)
    pallas_call x1, Pallas kernels, whole_block(): pl.pallas_call(block_kernel, out_shape=outs + tmp, in_specs=[vmem] * 2 +...  297 us

profile of v4, /device:TPU:1, one launch (start us, length us, event | category | flops | bytes accessed | tf_op | source)
XLA Modules:
  0.0 299.9 jit_solution(2916015492653653814)
XLA Ops:
  0.6 296.7 %whole_block.1 = (bf16[128,4096]{1,0:T(8,128)(2,1)}, bf16[16,4096]{1,0:T(8,128)(2,1)}, bf16[16,768]{1,0:T(8,128)(2,1)}, bf16[16,4096]{1,0:T(8,128)(2,1)}, bf16[1...) custom-call(s32[8,128]{1,0:T(8,128)} %bitcast.30, ...), custom_call_target="tpu_custom_call" | custom-call | tf_op jit(solution)/shard_map/whole_block/pallas_call | solution.py:684
  297.3 2.5 hand_over.1
